TPU v7x, 128 devices: a whole 4x4x4 slice. The times are simulated.
128 devices in a mesh: gx: 8 (over z, core), gy: 16 (over y, x).
Axes of the slice: x: 4, y: 4, z: 4, core: 2. Of those that a mesh axis runs over, the one named last changes fastest.
Arguments:
- velocity: float32 [3, 64, 512, 1024], P(None, None, 'gy', 'gx'), may hold values from -6 to 6
- pressure: float32 [64, 512, 1024], P(None, 'gy', 'gx'), may hold values from -6 to 6
- memory: float32 [64, 512, 1024], P(None, 'gy', 'gx'), may hold values from -4 to 4
- buoyancy: float32 [64, 512, 1024], P(None, 'gy', 'gx'), may hold values from 0.1 to 0.4
- modulus: float32 [64, 512, 1024], P(None, 'gy', 'gx'), may hold values from 0.1 to 0.4
- relax: float32 [64, 512, 1024], P(None, 'gy', 'gx'), may hold values from 0.05 to 0.5
- strength: float32 [64, 512, 1024], P(None, 'gy', 'gx'), may hold values from 0.2 to 1
- spectra: float32 [32768, 256], P(('gx', 'gy')), may hold values from -6 to 6
- patch_cell: int32 [32768], P(('gx', 'gy')), may hold values from 0 to 262143
- rupture_patches: int32 [64, 512], replicated, may hold values from -1 to 32767, as said below
- slip_weights: bfloat16 [64, 512, 512], P('gx', 'gy'), may hold values from -0.375 to 0.375
Outputs:
- velocity_out: float32 [3, 64, 512, 1024], P(None, None, 'gy', 'gx')
- pressure_out: float32 [64, 512, 1024], P(None, 'gy', 'gx')
- memory_out: float32 [64, 512, 1024], P(None, 'gy', 'gx')
- spectra_out: float32 [32768, 256], P(('gx', 'gy'))
- slip_response: float32 [64, 512, 256], P('gx', 'gy')
Inputs may be any that keep to these rules, and one draw needn't show every extreme that they name: `patch_cell`: the cell of a patch is a flat index (z * 32 + y) * 128 + x within its brick. `rupture_patches`: each patch is listed in at most one slot. Slot (r, s) belongs to the owner at index r // 8 of gx and s // 32 of gy; of the 256 patches of one block, at most 2 are listed in the slots of any one owner, and some pairs of block and owner reach 2.
All inputs are finite; a program needn't handle non-finite values.
Results may differ from a plain program's by a relative error of at most 0.0029.
Values may be sent and summed in bfloat16 or wider, within the bound.
No kernel may reach another device: no remote copies, remote signals or barrier semaphores. Data moves between devices by JAX's collectives and lax.ppermute only.
A program may use at most 128 MiB of HBM per device.

v0:
```python
import functools

import jax
import jax.numpy as jnp
from jax import lax
from jax.experimental import pallas as pl
from jax.experimental.pallas import tpu as pltpu
from jax.sharding import PartitionSpec as P

STEPS = 4
CAP = 2
NZ, NY, NX = 64, 32, 128
HALO = 8
EY = NY + 2 * HALO
FIELDS = 9
VX, VY, VZ, PR, ME, BU, MO, RE, ST = range(FIELDS)


def lanes(shape):
    return lax.broadcasted_iota(jnp.int32, shape, len(shape) - 1)


def roll(x, shift, axis=1):
    shift = shift % x.shape[axis]
    return pltpu.roll(x, shift, axis) if shift else x


def pack_kernel(vel, pr, me, bu, mo, re, st, lo_ref, hi_ref, q_ref):
    lane = lanes((NY, 128))
    fields = [vel.at[0], vel.at[1], vel.at[2], pr, me, bu, mo, re, st]
    for f, ref in enumerate(fields):
        lows, highs = [], []
        strip = jnp.zeros((NY, 128), jnp.float32)
        for g in range(8):
            plane = ref[g, 0]
            lows.append(plane[:HALO])
            highs.append(plane[NY - HALO :])
            strip = jnp.where((lane >> 4) == g, roll(plane, 8 + 16 * g), strip)
        lo_ref[0, f] = jnp.concatenate(lows, axis=0).astype(jnp.bfloat16)
        hi_ref[0, f] = jnp.concatenate(highs, axis=0).astype(jnp.bfloat16)
        q_ref[0, f] = strip.astype(jnp.bfloat16)


def pack(velocity, *fields):
    spec = pl.BlockSpec((8, 1, NY, NX), lambda i: (0, i, 0, 0))
    vspec = pl.BlockSpec((3, 8, 1, NY, NX), lambda i: (0, 0, i, 0, 0))
    yspec = pl.BlockSpec((1, FIELDS, 64, 128), lambda i: (i, 0, 0, 0))
    qspec = pl.BlockSpec((1, FIELDS, NY, 128), lambda i: (i, 0, 0, 0))
    yshape = jax.ShapeDtypeStruct((8, FIELDS, 64, 128), jnp.bfloat16)
    qshape = jax.ShapeDtypeStruct((8, FIELDS, NY, 128), jnp.bfloat16)
    return pl.pallas_call(
        pack_kernel,
        out_shape=(yshape, yshape, qshape),
        grid=(8,),
        in_specs=[vspec] + [spec] * 6,
        out_specs=(yspec, yspec, qspec),
        name="pack",
    )(velocity.reshape(3, 8, 8, NY, NX), *[f.reshape(8, 8, NY, NX) for f in fields])


def shifted(array, axis, up):
    n = lax.axis_size(axis)
    pairs = [(i, i + 1) if up else (i + 1, i) for i in range(n - 1)]
    return lax.ppermute(array, axis, pairs)


def swap_edges(x, low):
    return jnp.where(low, roll(x, -1), roll(x, 1))


def ydiff(x):
    return roll(x, -1, 0) - roll(x, 1, 0)


def steps_kernel(
    cell,
    vel,
    pr,
    me,
    bu,
    mo,
    re,
    st,
    spectra,
    phase,
    lane_of,
    yprev,
    ynext,
    side,
    cprev,
    cnext,
    vel_o,
    pr_o,
    me_o,
    spec_o,
    E,
    S,
    shear,
    G,
    sems,
):
    inside = pl.ds(HALO, NY)
    zin = pl.ds(1, NZ)
    sources = [vel.at[0], vel.at[1], vel.at[2], pr, me, bu, mo, re, st]
    copies = [
        pltpu.make_async_copy(src, E.at[f, zin, inside, :], sems.at[f])
        for f, src in enumerate(sources)
    ]
    for c in copies:
        c.start()
    lane = lanes((EY, 128))
    lane16 = lane & 15
    group = lane >> 4
    low = lane16 <= 7
    zero = jnp.zeros((EY, 128), jnp.float32)
    for f in (VZ, PR):
        E[f, 0] = zero
        E[f, NZ + 1] = zero

    def fill(zi, _):
        cp = cprev[zi].astype(jnp.float32)
        cn = cnext[zi].astype(jnp.float32)
        for f in range(FIELDS):
            yp = yprev[zi, f].astype(jnp.float32)
            yn = ynext[zi, f].astype(jnp.float32)
            for g in range(8):
                z = g * 8 + zi + 1
                E[f, z, :HALO] = yp[8 * g : 8 * g + 8]
                E[f, z, HALO + NY :] = yn[8 * g : 8 * g + 8]
            S[f, zi + 1, HALO : HALO + NY] = side[zi, f].astype(jnp.float32)
            S[f, zi + 1, :HALO] = cp[8 * f : 8 * f + 8]
            S[f, zi + 1, HALO + NY :] = cn[8 * f : 8 * f + 8]
        return 0

    lax.fori_loop(0, 8, fill, 0)

    def wrap_planes(f):
        S[f, 0] = jnp.where(lane < 16, 0.0, roll(S[f, 8], 16))
        S[f, 9] = jnp.where(lane >= 112, 0.0, roll(S[f, 1], -16))

    wrap_planes(PR)
    spec_o[...] = spectra[...]
    for c in copies:
        c.wait()

    def velocities(zi, _):
        zs = zi + 1
        edge = swap_edges(S[PR, zs], low)
        join = zero
        for g in range(8):
            z = g * 8 + zi + 1
            p0 = E[PR, z]
            halo = roll(edge, 120 - 16 * g)
            dx = jnp.where(lane == 127, halo, roll(p0, -1)) - jnp.where(lane == 0, halo, roll(p0, 1))
            b = E[BU, z]
            E[VX, z] = E[VX, z] - b * dx
            E[VY, z] = E[VY, z] - b * ydiff(p0)
            E[VZ, z] = E[VZ, z] - b * (E[PR, z + 1] - E[PR, z - 1])
            join = jnp.where(group == g, roll(p0, 16 * g + 8), join)
        join = swap_edges(join, low)
        ps = S[PR, zs]
        b = S[BU, zs]
        dx = jnp.where(lane16 == 7, join, roll(ps, -1)) - jnp.where(lane16 == 8, join, roll(ps, 1))
        S[VX, zs] = S[VX, zs] - b * dx
        S[VY, zs] = S[VY, zs] - b * ydiff(ps)
        S[VZ, zs] = S[VZ, zs] - b * (S[PR, zs + 1] - S[PR, zs - 1])
        return 0

    def updated(ref, z, spread):
        m = ref[ME, z]
        m = m - ref[RE, z] * (m + ref[ST, z] * spread)
        ref[ME, z] = m
        ref[PR, z] = ref[PR, z] - ref[MO, z] * (spread + m)

    def pressures(zi, _):
        zs = zi + 1
        edge_x = swap_edges(S[VX, zs], low)
        edge_y = swap_edges(S[VY, zs], low)[HALO : HALO + NY]
        join = zero
        lane_in = lane[:NY]
        for g in range(8):
            z = g * 8 + zi + 1
            vx, vy = E[VX, z], E[VY, z]
            halo = roll(edge_x, 120 - 16 * g)
            dx = jnp.where(lane == 127, halo, roll(vx, -1)) - jnp.where(lane == 0, halo, roll(vx, 1))
            spread = dx + ydiff(vy) + (E[VZ, z + 1] - E[VZ, z - 1])
            updated(E, z, spread)
            vy = vy[HALO : HALO + NY]
            halo = roll(edge_y, 120 - 16 * g)
            dx = jnp.where(lane_in == 127, halo, roll(vy, -1)) - jnp.where(
                lane_in == 0, halo, roll(vy, 1)
            )
            row = pl.multiple_of((g * 8 + zi) * NY, NY)
            shear[pl.ds(row, NY), :] = ydiff(vx)[HALO : HALO + NY] + dx
            join = jnp.where(group == g, roll(vx, 16 * g + 8), join)
        join = swap_edges(join, low)
        vx, vy = S[VX, zs], S[VY, zs]
        dx = jnp.where(lane16 == 7, join, roll(vx, -1)) - jnp.where(lane16 == 8, join, roll(vx, 1))
        updated(S, zs, dx + ydiff(vy) + (S[VZ, zs + 1] - S[VZ, zs - 1]))
        return 0

    wanted = lanes((256, 128)) == lane_of[...]

    def step(n, _):
        lax.fori_loop(0, 8, velocities, 0)
        wrap_planes(VZ)
        lax.fori_loop(0, 8, pressures, 0)
        wrap_planes(PR)

        def pick(i, _):
            for k in range(8):
                c = cell[i * 8 + k]
                G[pl.ds(i * 8 + k, 1), :] = shear[pl.ds(c >> 7, 1), :]
            return 0

        lax.fori_loop(0, 32, pick, 0)
        sample = jnp.sum(jnp.where(wanted, G[...], 0.0), axis=1, keepdims=True)
        spec_o[...] = spec_o[...] + sample * phase[pl.ds(n, 1), :]
        return 0

    lax.fori_loop(0, STEPS, step, 0)
    outs = [
        pltpu.make_async_copy(E.at[f, zin, inside, :], dst, sems.at[f])
        for f, dst in enumerate([vel_o.at[0], vel_o.at[1], vel_o.at[2], pr_o, me_o])
    ]
    for c in outs:
        c.start()
    for c in outs:
        c.wait()


def phase_rows(freqs):
    rows = []
    for step in range(1, STEPS + 1):
        angle = jnp.pi * (jnp.arange(freqs, dtype=jnp.float32) + 0.5) / freqs * step
        rows.append(jnp.concatenate([jnp.cos(angle), -jnp.sin(angle)]))
    return jnp.stack(rows)


def four_steps(velocity, fields, spectra, patch_cell, halos):
    any_spec = pl.BlockSpec(memory_space=pl.ANY)
    vmem = pl.BlockSpec(memory_space=pltpu.VMEM)
    smem = pl.BlockSpec(memory_space=pltpu.SMEM)
    field = jax.ShapeDtypeStruct((NZ, NY, NX), jnp.float32)
    return pl.pallas_call(
        steps_kernel,
        out_shape=(
            jax.ShapeDtypeStruct(velocity.shape, jnp.float32),
            field,
            field,
            jax.ShapeDtypeStruct(spectra.shape, jnp.float32),
        ),
        in_specs=[smem] + [any_spec] * 7 + [vmem] * 8,
        out_specs=(any_spec, any_spec, any_spec, vmem),
        scratch_shapes=[
            pltpu.VMEM((FIELDS, NZ + 2, EY, 128), jnp.float32),
            pltpu.VMEM((FIELDS, 10, EY, 128), jnp.float32),
            pltpu.VMEM((NZ * NY, 128), jnp.float32),
            pltpu.VMEM((256, 128), jnp.float32),
            pltpu.SemaphoreType.DMA((FIELDS,)),
        ],
        compiler_params=pltpu.CompilerParams(vmem_limit_bytes=40 * 1024 * 1024),
        name="four_steps",
    )(
        patch_cell,
        velocity,
        *fields,
        spectra,
        phase_rows(spectra.shape[1] // 2),
        (patch_cell & 127)[:, None],
        *halos,
    )


def halo_exchange(velocity, fields):
    lo, hi, q = pack(velocity, *fields)
    yprev = shifted(hi, "gy", True)
    ynext = shifted(lo, "gy", False)
    left = shifted(q, "gx", True)
    right = shifted(q, "gx", False)
    side = jnp.where((jnp.arange(128) & 15) < 8, left, right)
    cprev = shifted(side[:, :, NY - HALO :].reshape(8, FIELDS * HALO, 128), "gy", True)
    cnext = shifted(side[:, :, :HALO].reshape(8, FIELDS * HALO, 128), "gy", False)
    return yprev, ynext, side, cprev, cnext


def in_blocks(array, dim, peers):
    before, after = (array.shape[:dim], array.shape[dim + 1 :])
    return jnp.moveaxis(array.reshape(*before, peers, -1, *after), dim, 0)


def joined_along(parts, dim):
    parts = jnp.moveaxis(parts, 0, dim)
    lengths = parts.shape
    return parts.reshape(*lengths[:dim], lengths[dim] * lengths[dim + 1], *lengths[dim + 2 :])


def copy_for_each(array, axis):
    copies = jnp.broadcast_to(array, (lax.axis_size(axis), *array.shape))
    return lax.all_to_all(copies, axis, split_axis=0, concat_axis=0, tiled=True)


def slip_part(spectra, rupture_patches, slip_weights):
    freqs = spectra.shape[1] // 2
    groups_x = lax.axis_size("gx")
    groups_y = lax.axis_size("gy")
    devices = groups_x * groups_y
    owner = lax.axis_index("gx") * groups_y + lax.axis_index("gy")
    per_dev = spectra.shape[0]
    rup_group, slot_dev, variations = slip_weights.shape
    slots = rupture_patches.shape[1]
    flat_ids = rupture_patches.reshape(-1)
    slot_index = jnp.arange(flat_ids.shape[0], dtype=jnp.int32)
    target = slot_index // slots // rup_group * groups_y + slot_index % slots // slot_dev
    own_ids = owner * per_dev + jnp.arange(per_dev, dtype=jnp.int32)
    matches = flat_ids[None, :] == own_ids[:, None]
    target_of = jnp.max(jnp.where(matches, target[None, :], -1), axis=1)
    counter = jnp.arange(per_dev, dtype=jnp.int32)
    before = counter[None, :] < counter[:, None]
    rank = jnp.sum(((target_of[None, :] == target_of[:, None]) & before).astype(jnp.int32), axis=1)
    bucket = jnp.where(target_of >= 0, target_of * CAP + rank, -1)
    placing = (jnp.arange(devices * CAP, dtype=jnp.int32)[:, None] == bucket[None, :]).astype(
        jnp.bfloat16
    )
    rounded = spectra.astype(jnp.bfloat16)
    outgoing = jnp.dot(placing, rounded, preferred_element_type=jnp.float32).astype(jnp.bfloat16)
    received = lax.all_to_all(
        outgoing.reshape(devices, CAP, 2 * freqs), ("gx", "gy"), 0, 0, tiled=True
    ).reshape(devices * CAP, 2 * freqs)
    local_ids = lax.dynamic_slice(
        rupture_patches,
        (lax.axis_index("gx") * rup_group, lax.axis_index("gy") * slot_dev),
        (rup_group, slot_dev),
    ).reshape(-1)
    source = local_ids // per_dev
    earlier_slot = (
        (local_ids[None, :] < local_ids[:, None])
        & (source[None, :] == source[:, None])
        & (local_ids[None, :] >= 0)
    )
    rank_in = jnp.sum(earlier_slot.astype(jnp.int32), axis=1)
    live = local_ids >= 0
    row = jnp.where(live, source * CAP + rank_in, 0)
    picked = jnp.take(received, row, axis=0)
    slot_spectra = jnp.where(live[:, None], picked, jnp.zeros_like(picked)).reshape(
        rup_group, slot_dev, 2 * freqs
    )
    swapped = lax.all_to_all(slip_weights, "gy", split_axis=2, concat_axis=1, tiled=True)
    return jnp.einsum(
        "rsv,rsf->rvf",
        swapped,
        joined_along(copy_for_each(slot_spectra, "gy"), 1),
        preferred_element_type=jnp.float32,
    )


def per_device(
    velocity,
    pressure,
    memory,
    buoyancy,
    modulus,
    relax,
    strength,
    spectra,
    patch_cell,
    rupture_patches,
    slip_weights,
):
    fields = (pressure, memory, buoyancy, modulus, relax, strength)
    halos = halo_exchange(velocity, fields)
    velocity, pressure, memory, spectra = four_steps(velocity, fields, spectra, patch_cell, halos)
    slip = slip_part(spectra, rupture_patches, slip_weights)
    return (velocity, pressure, memory, spectra, slip)


def solution(mesh):
    field = P(None, "gy", "gx")
    in_specs = (
        (P(None, None, "gy", "gx"),)
        + (field,) * 6
        + (P(("gx", "gy"), None), P(("gx", "gy")), P(), P("gx", "gy", None))
    )
    out_specs = (
        P(None, None, "gy", "gx"),
        field,
        field,
        P(("gx", "gy"), None),
        P("gx", "gy", None),
    )
    return jax.shard_map(
        per_device, mesh=mesh, in_specs=in_specs, out_specs=out_specs, check_vma=False
    )
```

profile of v0, /device:TPU:1, one launch (start us, length us, event | category | flops | bytes accessed | tf_op | source)
XLA Modules:
  0.0 168.0 jit_solution(16410044566475211515)
XLA Ops:
  0.7 7.6 %pack.1 = (bf16[8,9,64,128]{3,2,1,0:T(8,128)(2,1)}, bf16[8,9,64,128]{3,2,1,0:T(8,128)(2,1)}, bf16[8,9,32,128]{3,2,1,0:T(8,128)(2,1)}) custom-call(f32[3,8,8,32,128]{4,3,2,1,0:T(8,128)} %bitcast.37, f32[8,8,32,128]{3,2,1,0:T(8,128)} %bitcast.38, f32[8,8,32,128]{3,2,1,0:T(8,128)} %bitcast.39, f32[8,8,32,128]{3,2,1,0:T(8,128)} %bitcast.40, ...), custom_call_target="tpu_custom_call" | custom-call | tf_op jit(solution)/shard_map/pack/pallas_call | solution.py:51
  8.3 4.9 %collective-permute-start.2 = (bf16[8,9,32,128]{3,2,1,0:T(8,128)(2,1)}, bf16[8,9,32,128]{3,2,1,0:T(8,128)(2,1)S(1)}, u32[]{:S(2)}, u32[]{:S(2)}) collective-permute-start(bf16[8,9,32,128]{3,2,1,0:T(8,128)(2,1)} %get-tuple-element.14), channel_id=1, source_target_pairs={{0,16},{16,32},{32,48},{48,64},{64,80},{80,96},{96,112},{1,17},{17... | collective-permute-start | bytes 1769480 | tf_op jit(solution)/shard_map/ppermute | solution.py:64
  13.2 1.9 %collective-permute-start.3 = (bf16[8,9,32,128]{3,2,1,0:T(8,128)(2,1)}, bf16[8,9,32,128]{3,2,1,0:T(8,128)(2,1)S(1)}, u32[]{:S(2)}, u32[]{:S(2)}) collective-permute-start(bf16[8,9,32,128]{3,2,1,0:T(8,128)(2,1)} %get-tuple-element.14), channel_id=1, source_target_pairs={{16,0},{32,16},{48,32},{64,48},{80,64},{96,80},{112,96},{17,1},{33... | collective-permute-start | bytes 1769480 | tf_op jit(solution)/shard_map/ppermute | solution.py:64
  15.1 4.1 %collective-permute-start = (bf16[8,9,64,128]{3,2,1,0:T(8,128)(2,1)}, bf16[8,9,64,128]{3,2,1,0:T(8,128)(2,1)}, u32[]{:S(2)}, u32[]{:S(2)}) collective-permute-start(bf16[8,9,64,128]{3,2,1,0:T(8,128)(2,1)} %get-tuple-element.12), channel_id=1, source_target_pairs={{0,1},{1,2},{2,3},{3,4},{4,5},{5,6},{6,7},{7,8},{8,9},{9,10},{10,1... | collective-permute-start | bytes 3538952 | tf_op jit(solution)/shard_map/ppermute | solution.py:64
  19.3 1.3 collective-permute-start.1
  21.7 4.6 %select_reduce_fusion = s32[256]{0:T(256)S(1)} fusion(s32[32768]{0:T(1024)S(1)} %fusion.9, s32[32768]{0:T(1024)S(1)} %bitcast.49, s32[256]{0:T(256)S(1)} %iota_add_fusion), kind=kLoop, calls=%fused_computation.1 | loop fusion | flops 25165568 | bytes 264192 | tf_op jit(solution)/shard_map/reduce_max | solution.py:317
  30.0 0.8 copy-done.7
  30.8 4.6 %collective-permute-start.4 = (bf16[8,72,128]{2,1,0:T(8,128)(2,1)}, bf16[8,72,128]{2,1,0:T(8,128)(2,1)}, u32[]{:S(2)}, u32[]{:S(2)}) collective-permute-start(bf16[8,72,128]{2,1,0:T(8,128)(2,1)} %get-tuple-element.22), channel_id=1, source_target_pairs={{0,1},{1,2},{2,3},{3,4},{4,5},{5,6},{6,7},{7,8},{8,9},{9,10},{10,1... | collective-permute-start | bytes 442376 | tf_op jit(solution)/shard_map/ppermute | solution.py:64
  35.5 1.3 collective-permute-start.5
  38.8 2.6 %copy.25 = bf16[8,32,512]{1,0,2:T(8,128)(2,1)} copy(bf16[8,32,512]{2,1,0:T(8,128)(2,1)} %param.21) | data formatting | bytes 524288 | tf_op args[10]
  41.5 3.1 %reshape.308 = bf16[16,2,4096]{2,1,0:T(2,128)(2,1)} reshape(bf16[512,8,32]{2,1,0:T(8,128)(2,1)} %bitcast.46) | data formatting | bytes 524288
  45.7 5.1 %collective-permute-done.5.cnext = bf16[8,72,128]{2,1,0:T(8,128)(2,1)} collective-permute-done((bf16[8,72,128]{2,1,0:T(8,128)(2,1)}, bf16[8,72,128]{2,1,0:T(8,128)(2,1)}, u32[]{:S(2)}, u32[]{:S(2)}) %collective-permute-start.5) | collective-permute-done | bytes 147488 | tf_op jit(solution)/shard_map/ppermute | solution.py:64
  50.8 1.2 copy-done.1
  52.0 1.2 copy-done.2
  53.3 1.2 copy-done.3
  54.5 1.2 copy-done.4
  55.7 1.2 copy-done.5
  56.9 1.2 copy-done.6
  58.2 1.1 copy-done.8
  59.2 37.0 %four_steps.1 = (f32[3,64,32,128]{3,2,1,0:T(8,128)}, f32[64,32,128]{2,1,0:T(8,128)}, f32[64,32,128]{2,1,0:T(8,128)}, f32[256,256]{1,0:T(8,128)}) custom-call(s32[256]{0:T(256)S(1)} %copy-done.10, f32[3,64,32,128]{3,2,1,0:T(8,128)S(1)} %copy-done, f32[64,32,128]{2,1,0:T(8,128)S(1)} %copy-done.1, f32[64,32,128]{2,1,0:T(8,128)S(1)} %copy-done.2, ...), custom_call_target="tpu_custom_call" | custom-call | tf_op jit(solution)/shard_map/four_steps/pallas_call | solution.py:245
  96.3 1.1 convolution_convert_fusion
  98.1 12.3 %all-to-all-start = ((bf16[128,2,256]{2,1,0:T(2,128)(2,1)}), bf16[128,2,256]{2,1,0:T(2,128)(2,1)S(1)}, u32[]{:S(2)}, u32[]{:S(2)}) async-start(bf16[128,2,256]{2,1,0:T(2,128)(2,1)} %reshape.296), calls=%async_computation | async-start | bytes 262144 | tf_op jit(solution)/shard_map/all_to_all | solution.py:327
  111.2 9.4 %all-to-all-done = bf16[128,2,256]{2,1,0:T(2,128)(2,1)S(1)} async-done(((bf16[128,2,256]{2,1,0:T(2,128)(2,1)}), bf16[128,2,256]{2,1,0:T(2,128)(2,1)S(1)}, u32[]{:S(2)}, u32[]{:S(2)}) %all-to-all-start) | async-done | bytes 131104 | tf_op jit(solution)/shard_map/all_to_all | solution.py:327
  120.5 3.5 %all-to-all-start.2 = ((bf16[16,2,4096]{2,1,0:T(2,128)(2,1)}), bf16[16,2,4096]{2,1,0:T(2,128)(2,1)S(1)}, u32[]{:S(2)}, u32[]{:S(2)}) async-start(bf16[16,2,4096]{2,1,0:T(2,128)(2,1)} %reshape.308), calls=%async_computation.2 | async-start | bytes 524288 | tf_op jit(solution)/shard_map/all_to_all | solution.py:348
  124.1 1.2 gather_fusion
  125.4 6.8 %all-to-all-done.2 = bf16[16,2,4096]{2,1,0:T(2,128)(2,1)S(1)} async-done(((bf16[16,2,4096]{2,1,0:T(2,128)(2,1)}), bf16[16,2,4096]{2,1,0:T(2,128)(2,1)S(1)}, u32[]{:S(2)}, u32[]{:S(2)}) %all-to-all-start.2) | async-done | bytes 262176 | tf_op jit(solution)/shard_map/all_to_all | solution.py:348
  132.2 1.6 broadcast_in_dim.65
  133.8 3.9 %all-to-all-start.1 = ((bf16[16,8,32,256]{3,2,1,0:T(8,128)(2,1)}), bf16[16,8,32,256]{3,2,1,0:T(8,128)(2,1)S(1)}, u32[]{:S(2)}, u32[]{:S(2)}) async-start(bf16[16,8,32,256]{3,2,1,0:T(8,128)(2,1)} %broadcast_in_dim.65), calls=%async_computation.1 | async-start | bytes 4194304 | tf_op jit(solution)/shard_map/all_to_all | solution.py:300
  138.2 1.7 copy.29
  139.9 2.2 %all_to_all.24 = bf16[8,512,32]{1,2,0:T(8,128)(2,1)S(1)} reshape(bf16[8,16,32,32]{2,1,3,0:T(8,128)(2,1)} %bitcast.48) | data formatting | bytes 524288 | tf_op jit(solution)/shard_map/all_to_all | solution.py:348
  142.1 24.5 %all-to-all-done.1 = bf16[16,8,32,256]{3,2,1,0:T(8,128)(2,1)S(1)} async-done(((bf16[16,8,32,256]{3,2,1,0:T(8,128)(2,1)}), bf16[16,8,32,256]{3,2,1,0:T(8,128)(2,1)S(1)}, u32[]{:S(2)}, u32[]{:S(2)}) %all-to-all-start.1) | async-done | bytes 2097184 | tf_op jit(solution)/shard_map/all_to_all | solution.py:300
  166.8 1.2 convolution_bitcast_fusion
  (57 shorter events, 10.3 us)
Async XLA Ops:
  0.6 19.9 %copy-start.11 = (s32[64,512]{1,0:T(8,128)S(1)}, s32[64,512]{1,0:T(8,128)}, u32[]{:S(2)}) copy-start(s32[64,512]{1,0:T(8,128)} %param.20) | copy-start | bytes 393220
  0.6 20.4 %copy-start.10 = (s32[256]{0:T(256)S(1)}, s32[256]{0:T(256)}, u32[]{:S(2)}) copy-start(s32[256]{0:T(256)} %cell.1) | copy-start | bytes 3076
  8.3 20.9 %collective-permute-start.2 = (bf16[8,9,32,128]{3,2,1,0:T(8,128)(2,1)}, bf16[8,9,32,128]{3,2,1,0:T(8,128)(2,1)S(1)}, u32[]{:S(2)}, u32[]{:S(2)}) collective-permute-start(bf16[8,9,32,128]{3,2,1,0:T(8,128)(2,1)} %get-tuple-element.14), channel_id=1, source_target_pairs={{0,16},{16,32},{32,48},{48,64},{64,80},{80,96},{96,112},{1,17},{17... | collective-permute-start | bytes 1769480 | tf_op jit(solution)/shard_map/ppermute | solution.py:64
  13.2 15.9 %collective-permute-start.3 = (bf16[8,9,32,128]{3,2,1,0:T(8,128)(2,1)}, bf16[8,9,32,128]{3,2,1,0:T(8,128)(2,1)S(1)}, u32[]{:S(2)}, u32[]{:S(2)}) collective-permute-start(bf16[8,9,32,128]{3,2,1,0:T(8,128)(2,1)} %get-tuple-element.14), channel_id=1, source_target_pairs={{16,0},{32,16},{48,32},{64,48},{80,64},{96,80},{112,96},{17,1},{33... | collective-permute-start | bytes 1769480 | tf_op jit(solution)/shard_map/ppermute | solution.py:64
  15.1 35.7 %collective-permute-start = (bf16[8,9,64,128]{3,2,1,0:T(8,128)(2,1)}, bf16[8,9,64,128]{3,2,1,0:T(8,128)(2,1)}, u32[]{:S(2)}, u32[]{:S(2)}) collective-permute-start(bf16[8,9,64,128]{3,2,1,0:T(8,128)(2,1)} %get-tuple-element.12), channel_id=1, source_target_pairs={{0,1},{1,2},{2,3},{3,4},{4,5},{5,6},{6,7},{7,8},{8,9},{9,10},{10,1... | collective-permute-start | bytes 3538952 | tf_op jit(solution)/shard_map/ppermute | solution.py:64
  19.3 31.5 %collective-permute-start.1 = (bf16[8,9,64,128]{3,2,1,0:T(8,128)(2,1)}, bf16[8,9,64,128]{3,2,1,0:T(8,128)(2,1)}, u32[]{:S(2)}, u32[]{:S(2)}) collective-permute-start(bf16[8,9,64,128]{3,2,1,0:T(8,128)(2,1)} %get-tuple-element.13), channel_id=1, source_target_pairs={{1,0},{2,1},{3,2},{4,3},{5,4},{6,5},{7,6},{8,7},{9,8},{10,9},{11,1... | collective-permute-start | bytes 3538952 | tf_op jit(solution)/shard_map/ppermute | solution.py:64
  29.2 21.6 %copy-start.9 = (f32[256,256]{1,0:T(8,128)S(1)}, f32[256,256]{1,0:T(8,128)}, u32[]{:S(2)}) copy-start(f32[256,256]{1,0:T(8,128)} %spectra.1) | copy-start | bytes 786436
  29.2 21.6 %copy-start = (f32[3,64,32,128]{3,2,1,0:T(8,128)S(1)}, f32[3,64,32,128]{3,2,1,0:T(8,128)}, u32[]{:S(2)}) copy-start(f32[3,64,32,128]{3,2,1,0:T(8,128)} %vel.1) | copy-start | bytes 9437188
  30.0 0.8 copy-start.7
  30.8 14.9 %collective-permute-start.4 = (bf16[8,72,128]{2,1,0:T(8,128)(2,1)}, bf16[8,72,128]{2,1,0:T(8,128)(2,1)}, u32[]{:S(2)}, u32[]{:S(2)}) collective-permute-start(bf16[8,72,128]{2,1,0:T(8,128)(2,1)} %get-tuple-element.22), channel_id=1, source_target_pairs={{0,1},{1,2},{2,3},{3,4},{4,5},{5,6},{6,7},{7,8},{8,9},{9,10},{10,1... | collective-permute-start | bytes 442376 | tf_op jit(solution)/shard_map/ppermute | solution.py:64
  35.5 15.3 %collective-permute-start.5 = (bf16[8,72,128]{2,1,0:T(8,128)(2,1)}, bf16[8,72,128]{2,1,0:T(8,128)(2,1)}, u32[]{:S(2)}, u32[]{:S(2)}) collective-permute-start(bf16[8,72,128]{2,1,0:T(8,128)(2,1)} %get-tuple-element.21), channel_id=1, source_target_pairs={{1,0},{2,1},{3,2},{4,3},{5,4},{6,5},{7,6},{8,7},{9,8},{10,9},{11,1... | collective-permute-start | bytes 442376 | tf_op jit(solution)/shard_map/ppermute | solution.py:64
  44.5 51.8 %copy-start.12 = (s32[256]{0:T(256)S(1)}, s32[256]{0:T(256)}, u32[]{:S(2)}) copy-start(s32[256]{0:T(256)} %compare_select_fusion.6) | copy-start | bytes 3076
  50.8 1.2 copy-start.1
  52.0 1.2 copy-start.2
  53.3 1.2 copy-start.3
  54.5 1.2 copy-start.4
  55.7 1.2 copy-start.5
  56.9 1.2 copy-start.6
  58.2 1.1 copy-start.8
  98.1 22.4 %all-to-all-start = ((bf16[128,2,256]{2,1,0:T(2,128)(2,1)}), bf16[128,2,256]{2,1,0:T(2,128)(2,1)S(1)}, u32[]{:S(2)}, u32[]{:S(2)}) async-start(bf16[128,2,256]{2,1,0:T(2,128)(2,1)} %reshape.296), calls=%async_computation | async-start | bytes 262144 | tf_op jit(solution)/shard_map/all_to_all | solution.py:327
  120.5 11.7 %all-to-all-start.2 = ((bf16[16,2,4096]{2,1,0:T(2,128)(2,1)}), bf16[16,2,4096]{2,1,0:T(2,128)(2,1)S(1)}, u32[]{:S(2)}, u32[]{:S(2)}) async-start(bf16[16,2,4096]{2,1,0:T(2,128)(2,1)} %reshape.308), calls=%async_computation.2 | async-start | bytes 524288 | tf_op jit(solution)/shard_map/all_to_all | solution.py:348
  133.8 32.8 %all-to-all-start.1 = ((bf16[16,8,32,256]{3,2,1,0:T(8,128)(2,1)}), bf16[16,8,32,256]{3,2,1,0:T(8,128)(2,1)S(1)}, u32[]{:S(2)}, u32[]{:S(2)}) async-start(bf16[16,8,32,256]{3,2,1,0:T(8,128)(2,1)} %broadcast_in_dim.65), calls=%async_computation.1 | async-start | bytes 4194304 | tf_op jit(solution)/shard_map/all_to_all | solution.py:300
where the time goes:
time: 170 us; the launch traced here: 168 us
  waiting for transfers between devices  46.2 us (27%)
  Pallas kernels  44.7 us (26%)
  starting transfers between devices  37.9 us (22%)
  local copies, waits for them, and re-layouts  25.4 us (15%)
  other arithmetic  10.5 us (6%)
  matrix products  2.31 us (1%)
    pallas_call x1, Pallas kernels, four_steps(): pl.pallas_call(steps_kernel, out_shape=(jax.ShapeDtypeStruct(velocity.sha...  37 us
    all_to_all x1, waiting for transfers between devices, copy_for_each(): return lax.all_to_all(copies, axis, split_axis=0, concat_axis=0, tiled=True)  24.5 us
    ppermute x6, starting transfers between devices, shifted(): return lax.ppermute(array, axis, pairs)  18.2 us
    unnamed x30, local copies, waits for them, and re-layouts  15.5 us
    all_to_all x1, starting transfers between devices, slip_part(): lax.all_to_all(outgoing.reshape(devices, CAP, 2 * freqs), ('gx', 'gy'), 0...  12.3 us
    all_to_all x1, waiting for transfers between devices, slip_part(): lax.all_to_all(outgoing.reshape(devices, CAP, 2 * freqs), ('gx', 'gy'), 0...  9.36 us
    pallas_call x1, Pallas kernels, pack(): pl.pallas_call(pack_kernel, out_shape=(yshape, yshape, qshape), grid=(8,)...  7.63 us
    all_to_all x1, waiting for transfers between devices, slip_part(): lax.all_to_all(slip_weights, 'gy', split_axis=2, concat_axis=1, tiled=True)  6.77 us
  transfers between devices with their start and end apart: 9, of which 5 were waited for; matrix products, arithmetic and copies ran while one was open for 13% of the time, Pallas kernels for 0%

commit v1 on v0

v1 whole, which is shorter than its diff:
```python
import functools

import jax
import jax.numpy as jnp
from jax import lax
from jax.experimental import pallas as pl
from jax.experimental.pallas import tpu as pltpu
from jax.sharding import PartitionSpec as P

STEPS = 4
CAP = 2
NZ, NY, NX = 64, 32, 128
HALO = 8
EY = NY + 2 * HALO
FIELDS = 9
VX, VY, VZ, PR, ME, BU, MO, RE, ST = range(FIELDS)
BP = FIELDS


def lanes(shape):
    return lax.broadcasted_iota(jnp.int32, shape, len(shape) - 1)


def roll(x, shift, axis=1):
    shift = shift % x.shape[axis]
    return pltpu.roll(x, shift, axis) if shift else x


def pack_kernel(vel, pr, me, bu, mo, re, st, lo_ref, hi_ref, q_ref):
    lane = lanes((NY, 128))
    fields = [vel.at[0], vel.at[1], vel.at[2], pr, me, bu, mo, re, st]
    for f, ref in enumerate(fields):
        lows, highs = [], []
        strip = jnp.zeros((NY, 128), jnp.float32)
        for g in range(8):
            plane = ref[g, 0]
            turned = roll(plane, 8 + 16 * g)
            strip = jnp.where((lane >> 4) == g, turned, strip)
            ends = turned[:HALO], turned[NY - HALO :]
            if f == VX:
                ends = tuple(roll(e, -1) for e in ends)
            lows.append(ends[0])
            highs.append(ends[1])
        lo_ref[0, f] = jnp.concatenate(lows, axis=0).astype(jnp.bfloat16)
        hi_ref[0, f] = jnp.concatenate(highs, axis=0).astype(jnp.bfloat16)
        q_ref[0, f] = strip.astype(jnp.bfloat16)


def pack(velocity, *fields):
    spec = pl.BlockSpec((8, 1, NY, NX), lambda i: (0, i, 0, 0))
    vspec = pl.BlockSpec((3, 8, 1, NY, NX), lambda i: (0, 0, i, 0, 0))
    yspec = pl.BlockSpec((1, FIELDS, 64, 128), lambda i: (i, 0, 0, 0))
    qspec = pl.BlockSpec((1, FIELDS, NY, 128), lambda i: (i, 0, 0, 0))
    yshape = jax.ShapeDtypeStruct((8, FIELDS, 64, 128), jnp.bfloat16)
    qshape = jax.ShapeDtypeStruct((8, FIELDS, NY, 128), jnp.bfloat16)
    return pl.pallas_call(
        pack_kernel,
        out_shape=(yshape, yshape, qshape),
        grid=(8,),
        in_specs=[vspec] + [spec] * 6,
        out_specs=(yspec, yspec, qspec),
        name="pack",
    )(velocity.reshape(3, 8, 8, NY, NX), *[f.reshape(8, 8, NY, NX) for f in fields])


def shifted(array, axis, up):
    n = lax.axis_size(axis)
    pairs = [(i, i + 1) if up else (i + 1, i) for i in range(n - 1)]
    return lax.ppermute(array, axis, pairs)


def ydiff(x):
    return roll(x, -1, 0) - roll(x, 1, 0)


def turned_diff(x, other, at):
    return roll(jnp.where(at == 8, other, x), -2) - jnp.where(at == 7, other, x)


def back_diff(x, other, at):
    return jnp.where(at == 7, other, x) - roll(jnp.where(at == 6, other, x), 2)


def steps_kernel(
    cell,
    vel,
    pr,
    me,
    bu,
    mo,
    re,
    st,
    spectra,
    phase,
    lane_of,
    yprev,
    ynext,
    side,
    cprev,
    cnext,
    vel_o,
    pr_o,
    me_o,
    spec_o,
    samp_o,
    E,
    S,
    X,
    shear,
    G,
    sems,
):
    sources = [vel.at[0], vel.at[1], vel.at[2], pr, me, bu, mo, re, st]
    copies = [
        [pltpu.make_async_copy(src.at[:, zi], X.at[f, :, zi], sems.at[f, zi]) for f, src in enumerate(sources)]
        for zi in range(8)
    ]
    for row in copies:
        for c in row:
            c.start()
    lane = lanes((EY, 128))
    lane16 = lane & 15
    group = lane >> 4
    zero = jnp.zeros((EY, 128), jnp.float32)

    def fill(zi):
        cp = cprev[zi].astype(jnp.float32)
        cn = cnext[zi].astype(jnp.float32)
        for f in range(FIELDS):
            yp = yprev[zi, f].astype(jnp.float32)
            yn = ynext[zi, f].astype(jnp.float32)
            for g in range(8):
                z = g * 10 + zi + 1
                low, high = yp[8 * g : 8 * g + 8], yn[8 * g : 8 * g + 8]
                mid = roll(X[f, g, zi], (7 if f == VX else 8) + 16 * g)
                E[f, z, :HALO] = low
                E[f, z, HALO + NY :] = high
                E[f, z, HALO : HALO + NY] = mid
                if f == BU:
                    E[BP, z, :HALO] = roll(low, -1)
                    E[BP, z, HALO + NY :] = roll(high, -1)
                    E[BP, z, HALO : HALO + NY] = roll(mid, -1)
            low, high = cp[8 * f : 8 * f + 8], cn[8 * f : 8 * f + 8]
            mid = side[zi, f].astype(jnp.float32)
            if f in (VX, BU):
                to = VX if f == VX else BP
                S[to, zi + 1, :HALO] = roll(low, -1)
                S[to, zi + 1, HALO + NY :] = roll(high, -1)
                S[to, zi + 1, HALO : HALO + NY] = roll(mid, -1)
            if f != VX:
                S[f, zi + 1, :HALO] = low
                S[f, zi + 1, HALO + NY :] = high
                S[f, zi + 1, HALO : HALO + NY] = mid

    def wrap_planes(f):
        S[f, 0] = jnp.where(lane < 16, 0.0, roll(S[f, 8], 16))
        S[f, 9] = jnp.where(lane >= 112, 0.0, roll(S[f, 1], -16))
        for g in range(8):
            E[f, 10 * g] = roll(E[f, 10 * g - 2], 16) if g else zero
            E[f, 10 * g + 9] = roll(E[f, 10 * g + 11], -16) if g < 7 else zero

    spec_o[...] = spectra[...]
    samp_o[...] = jnp.zeros_like(samp_o)
    for zi in range(8):
        for c in copies[zi]:
            c.wait()
        fill(zi)
    wrap_planes(PR)

    def moved(ref, z, dx, p):
        ref[VX, z] = ref[VX, z] - ref[BP, z] * dx
        b = ref[BU, z]
        ref[VY, z] = ref[VY, z] - b * ydiff(p)
        ref[VZ, z] = ref[VZ, z] - b * (ref[PR, z + 1] - ref[PR, z - 1])

    def velocities(zi, _):
        zs = zi + 1
        ps = S[PR, zs]
        join = zero
        for g in range(8):
            z = g * 10 + zi + 1
            p = E[PR, z]
            moved(E, z, turned_diff(p, ps, lane - 16 * g), p)
            join = jnp.where(group == g, p, join)
        moved(S, zs, turned_diff(ps, join, lane16), ps)
        return 0

    def updated(ref, z, spread):
        m = ref[ME, z]
        m = m - ref[RE, z] * (m + ref[ST, z] * spread)
        ref[ME, z] = m
        ref[PR, z] = ref[PR, z] - ref[MO, z] * (spread + m)

    def pressures(zi, _):
        zs = zi + 1
        svx, svy = S[VX, zs], S[VY, zs]
        svy_in = svy[HALO : HALO + NY]
        lane_in = lane[:NY]
        join = zero
        for g in range(8):
            z = g * 10 + zi + 1
            vx, vy = E[VX, z], E[VY, z]
            spread = back_diff(vx, svx, lane - 16 * g) + ydiff(vy)
            updated(E, z, spread + (E[VZ, z + 1] - E[VZ, z - 1]))
            row = pl.multiple_of((g * 8 + zi) * NY, NY)
            shear[pl.ds(row, NY), :] = ydiff(vx)[HALO : HALO + NY] + turned_diff(
                vy[HALO : HALO + NY], svy_in, lane_in - 16 * g
            )
            join = jnp.where(group == g, vx, join)
        spread = back_diff(svx, join, lane16) + ydiff(svy)
        updated(S, zs, spread + (S[VZ, zs + 1] - S[VZ, zs - 1]))
        return 0

    wanted = lanes((256, 128)) == lane_of[...]

    def step(n, _):
        lax.fori_loop(0, 8, velocities, 0)
        wrap_planes(VZ)
        lax.fori_loop(0, 8, pressures, 0)
        wrap_planes(PR)

        def pick(i, _):
            for k in range(8):
                c = cell[i * 8 + k]
                G[pl.ds(i * 8 + k, 1), :] = shear[pl.ds(c >> 7, 1), :]
            return 0

        lax.fori_loop(0, 32, pick, 0)
        sample = jnp.sum(jnp.where(wanted, G[...], 0.0), axis=1, keepdims=True)
        spec_o[...] = spec_o[...] + sample * phase[pl.ds(n, 1), :]
        samp_o[...] = jnp.where(lanes((256, 128)) == n, sample, samp_o[...])
        return 0

    lax.fori_loop(0, STEPS, step, 0)
    targets = [vel_o.at[0], vel_o.at[1], vel_o.at[2], pr_o, me_o]
    outs = []
    for zi in range(8):
        for f, dst in enumerate(targets):
            for g in range(8):
                plane = E[f, g * 10 + zi + 1, HALO : HALO + NY]
                X[f, g, zi] = roll(plane, -(7 if f == VX else 8) - 16 * g)
            outs.append(pltpu.make_async_copy(X.at[f, :, zi], dst.at[:, zi], sems.at[f, zi]))
            outs[-1].start()
    for c in outs:
        c.wait()


def phase_rows(freqs):
    rows = []
    for step in range(1, STEPS + 1):
        angle = jnp.pi * (jnp.arange(freqs, dtype=jnp.float32) + 0.5) / freqs * step
        rows.append(jnp.concatenate([jnp.cos(angle), -jnp.sin(angle)]))
    return jnp.stack(rows)


def four_steps(velocity, fields, spectra, patch_cell, halos):
    any_spec = pl.BlockSpec(memory_space=pl.ANY)
    vmem = pl.BlockSpec(memory_space=pltpu.VMEM)
    smem = pl.BlockSpec(memory_space=pltpu.SMEM)
    field = jax.ShapeDtypeStruct((8, 8, NY, NX), jnp.float32)
    vel, pr, me, spec, samples = pl.pallas_call(
        steps_kernel,
        out_shape=(
            jax.ShapeDtypeStruct((3, 8, 8, NY, NX), jnp.float32),
            field,
            field,
            jax.ShapeDtypeStruct(spectra.shape, jnp.float32),
            jax.ShapeDtypeStruct((spectra.shape[0], 128), jnp.float32),
        ),
        in_specs=[smem] + [any_spec] * 7 + [vmem] * 8,
        out_specs=(any_spec, any_spec, any_spec, vmem, vmem),
        scratch_shapes=[
            pltpu.VMEM((FIELDS + 1, 80, EY, 128), jnp.float32),
            pltpu.VMEM((FIELDS + 1, 10, EY, 128), jnp.float32),
            pltpu.VMEM((FIELDS, 8, 8, NY, 128), jnp.float32),
            pltpu.VMEM((NZ * NY, 128), jnp.float32),
            pltpu.VMEM((256, 128), jnp.float32),
            pltpu.SemaphoreType.DMA((FIELDS, 8)),
        ],
        compiler_params=pltpu.CompilerParams(vmem_limit_bytes=56 * 1024 * 1024),
        name="four_steps",
    )(
        patch_cell,
        velocity.reshape(3, 8, 8, NY, NX),
        *[f.reshape(8, 8, NY, NX) for f in fields],
        spectra,
        phase_rows(spectra.shape[1] // 2),
        ((patch_cell + 7 + 16 * (patch_cell >> 15)) & 127)[:, None],
        *halos,
    )
    shape = (NZ, NY, NX)
    return vel.reshape(velocity.shape), pr.reshape(shape), me.reshape(shape), spec, samples


def halo_exchange(velocity, fields):
    lo, hi, q = pack(velocity, *fields)
    yprev = shifted(hi, "gy", True)
    ynext = shifted(lo, "gy", False)
    left = shifted(q, "gx", True)
    right = shifted(q, "gx", False)
    side = jnp.where((jnp.arange(128) & 15) < 8, left, right)
    cprev = shifted(side[:, :, NY - HALO :].reshape(8, FIELDS * HALO, 128), "gy", True)
    cnext = shifted(side[:, :, :HALO].reshape(8, FIELDS * HALO, 128), "gy", False)
    return yprev, ynext, side, cprev, cnext


def rows_of(shape):
    return lax.broadcasted_iota(jnp.int32, shape, 0)


def transposed_dot(a, b):
    return lax.dot_general(a, b, (((0,), (0,)), ((), ())), preferred_element_type=jnp.float32)


def as_row(column, n):
    eye = rows_of((n, n)) == lanes((n, n))
    return jnp.sum(jnp.where(eye, column, 0.0), axis=0, keepdims=True)


def as_column(row, n):
    eye = rows_of((n, n)) == lanes((n, n))
    return jnp.sum(jnp.where(eye, row, 0.0), axis=1, keepdims=True)


def route_kernel(where, table, spectra, weights, send, place, pick, hot, turned, stage):
    n = spectra.shape[0]
    gx, gy = where[0], where[1]
    base = (gx * 16 + gy) * n
    mine = table[pl.ds(pl.multiple_of(gx * 8, 8), 8), :].astype(jnp.float32)
    mine = pltpu.roll(mine, lax.rem(512 - 32 * gy, 512), 1)[:, :128]
    quarter = lanes((1, 128)) >> 5
    halves = []
    for h in range(2):
        half = jnp.zeros((1, 128), jnp.float32)
        for q in range(4):
            r = 4 * h + q
            half = jnp.where(quarter == q, roll(mine, 32 * q)[r : r + 1], half)
        halves.append(half)
    ids_r = jnp.concatenate(halves, axis=1)
    ids = as_column(ids_r, n).astype(jnp.int32)
    ids_r = ids_r.astype(jnp.int32)
    columns = []
    for chunk in range(n // 32):
        own = base + chunk * 32 + rows_of((32, 512))

        def search(r8, found):
            for k in range(8):
                r = r8 * 8 + k
                found = jnp.where(table[pl.ds(r, 1), :] == own, r, found)
            return found

        found = lax.fori_loop(0, table.shape[0] // 8, search, jnp.full((32, 512), -1, jnp.int32))
        slot = jnp.where(found >= 0, found * 512 + lanes((32, 512)), -1).astype(jnp.float32)
        columns.append(jnp.max(slot, axis=1, keepdims=True))
    slot = jnp.concatenate(columns, axis=0).astype(jnp.int32)
    rupture = slot >> 9
    target = (((rupture >> 3) << 4) + ((slot & 511) >> 5)).astype(jnp.float32)
    hot[...] = (lanes((n, 128)) == rupture).astype(jnp.float32).astype(jnp.bfloat16)
    target_row = as_row(target, n)
    before = rows_of((n, n)) < lanes((n, n))
    rank = jnp.sum(
        jnp.where((target == target_row) & before, 1.0, 0.0), axis=0, keepdims=True
    )
    same = (ids >> 8) == (ids_r >> 8)
    rank_in = jnp.sum(jnp.where(same & (ids < ids_r), 1.0, 0.0), axis=0, keepdims=True)
    device = rows_of((128, n))
    target_row = target_row.astype(jnp.int32)
    source_row = ids_r >> 8
    stage[...] = jnp.zeros_like(stage)
    rounded = spectra[...].astype(jnp.bfloat16)
    for k in range(CAP):
        to = jnp.where((device == target_row) & (rank == k), 1.0, 0.0).astype(jnp.bfloat16)
        back = jnp.where((device == source_row) & (rank_in == k), 1.0, 0.0).astype(jnp.bfloat16)
        place[k] = to
        pick[k] = back
        sent = jnp.dot(to, rounded, preferred_element_type=jnp.float32)
        sent_w = jnp.dot(back, weights[...], preferred_element_type=jnp.float32)
        for c in range(2):
            stage[:, 6 * k + c, :] = sent[:, 128 * c : 128 * (c + 1)]
        for c in range(4):
            stage[:, 6 * k + 2 + c, :] = sent_w[:, 128 * c : 128 * (c + 1)]
    send[...] = stage[...].astype(jnp.bfloat16)
    eye = (rows_of((n, n)) == lanes((n, n))).astype(jnp.float32).astype(jnp.bfloat16)
    turned[...] = transposed_dot(weights[...], eye).astype(jnp.bfloat16).reshape(turned.shape)


def sort_kernel(received, place, pick, turned, message, patch_weights, stage):
    stage[...] = received[...].astype(jnp.float32)
    spectra = jnp.zeros((256, 256), jnp.float32)
    mine = jnp.zeros((256, 512), jnp.float32)
    for k in range(CAP):
        parts = [stage[:, 6 * k + c, :].astype(jnp.bfloat16) for c in range(6)]
        spectra += transposed_dot(pick[k], jnp.concatenate(parts[:2], axis=1))
        mine += transposed_dot(place[k], jnp.concatenate(parts[2:], axis=1))
    patch_weights[...] = mine.astype(jnp.bfloat16)
    for j in range(16):
        message[j, :256] = spectra.astype(jnp.bfloat16)
        message[j, 256:] = turned[j]


def sums_kernel(samples, hot, patch_weights, out):
    lane = lanes((256, 128))
    sums = []
    listed = hot[...].astype(jnp.float32)
    for n in range(STEPS):
        sample = jnp.sum(jnp.where(lane == n, samples[...], 0.0), axis=1, keepdims=True)
        scaled = listed * sample
        high = scaled.astype(jnp.bfloat16)
        rest = (scaled - high.astype(jnp.float32)).astype(jnp.bfloat16).astype(jnp.float32)
        both = scaled.astype(jnp.bfloat16).astype(jnp.float32) + roll(rest, 64)
        total = transposed_dot(both.astype(jnp.bfloat16), patch_weights[...])
        sums.append(total[:64] + total[64:])
    quarter = lanes((64, 128)) >> 5
    for j in range(16):
        block = slice(128 * (j // 4), 128 * (j // 4) + 128)
        packed = jnp.zeros((64, 128), jnp.float32)
        for n in range(STEPS):
            packed = jnp.where(quarter == n, roll(sums[n][:, block], 32 * (n - j % 4)), packed)
        out[:, j] = packed.reshape(8, 8, 128)


def slip_kernel(gathered, sums, phase, out):
    total = jnp.sum(sums[...], axis=0)
    own = (lanes((32, 128)) & 31) == rows_of((32, 128))
    left = jnp.concatenate(
        [jnp.where(own, total[r : r + 1], 0.0) for r in range(8)], axis=0
    )
    slip = jnp.dot(
        left, phase[...], precision=lax.Precision.HIGHEST, preferred_element_type=jnp.float32
    )
    square = (256, 256)
    same = ((rows_of(square) >> 5) == (lanes(square) >> 5)).astype(jnp.float32)
    same = same.astype(jnp.bfloat16)
    for j in range(16):
        spread = jnp.concatenate([gathered[j, 256:]] * 8, axis=0) * same
        slip += jnp.dot(spread, gathered[j, :256], preferred_element_type=jnp.float32)
    out[...] = slip.reshape(out.shape)


def small_call(kernel, outs, name, scratch=(), smem=0, inputs=0):
    vmem = pl.BlockSpec(memory_space=pltpu.VMEM)
    specs = [pl.BlockSpec(memory_space=pltpu.SMEM)] * smem + [vmem] * (inputs - smem)
    shapes = tuple(jax.ShapeDtypeStruct(s, d) for s, d in outs)
    return pl.pallas_call(
        kernel,
        out_shape=shapes,
        in_specs=specs,
        out_specs=(vmem,) * len(shapes),
        scratch_shapes=scratch,
        name=name,
    )


def routed(spectra, rupture_patches, slip_weights):
    bf16, f32 = jnp.bfloat16, jnp.float32
    where = jnp.stack([lax.axis_index("gx"), lax.axis_index("gy")])
    tiles = (128, 16, 128)
    return small_call(
        route_kernel,
        [
            (tiles, bf16),
            ((2, 128, 256), bf16),
            ((2, 128, 256), bf16),
            ((256, 128), bf16),
            ((16, 32, 256), bf16),
        ],
        "route",
        [pltpu.VMEM(tiles, f32)],
        1,
        4,
    )(where, rupture_patches, spectra, slip_weights.reshape(256, 512))


def sorted_rows(received, place, pick, turned):
    return small_call(
        sort_kernel,
        [((16, 288, 256), jnp.bfloat16), ((256, 512), jnp.bfloat16)],
        "sort",
        [pltpu.VMEM(received.shape, jnp.float32)],
        0,
        4,
    )(received, place, pick, turned)


def slip_response(gathered, patch_weights, hot, samples):
    f32 = jnp.float32
    (sums,) = small_call(sums_kernel, [((8, 16, 8, 128), f32)], "sums", (), 0, 3)(
        samples, hot, patch_weights
    )
    sums = lax.all_to_all(sums.reshape(128, 8, 128), ("gx", "gy"), 0, 0, tiled=True)
    phase = jnp.repeat(phase_rows(128), 32, axis=0)
    (slip,) = small_call(slip_kernel, [((8, 32, 256), f32)], "slip", (), 0, 3)(
        gathered, sums, phase
    )
    return slip


def per_device(
    velocity,
    pressure,
    memory,
    buoyancy,
    modulus,
    relax,
    strength,
    spectra,
    patch_cell,
    rupture_patches,
    slip_weights,
):
    fields = (pressure, memory, buoyancy, modulus, relax, strength)
    halos = halo_exchange(velocity, fields)
    send, place, pick, hot, turned = routed(spectra, rupture_patches, slip_weights)
    received = lax.all_to_all(send, ("gx", "gy"), 0, 0, tiled=True)
    received, _ = lax.optimization_barrier((received, halos))
    message, patch_weights = sorted_rows(received, place, pick, turned)
    gathered = lax.all_to_all(message, "gy", 0, 0, tiled=True)
    spectra, message = lax.optimization_barrier((spectra, message))
    velocity, pressure, memory, spectra, samples = four_steps(
        velocity, fields, spectra, patch_cell, halos
    )
    samples, gathered = lax.optimization_barrier((samples, gathered))
    slip = slip_response(gathered, patch_weights, hot, samples)
    return (velocity, pressure, memory, spectra, slip)


def solution(mesh):
    field = P(None, "gy", "gx")
    in_specs = (
        (P(None, None, "gy", "gx"),)
        + (field,) * 6
        + (P(("gx", "gy"), None), P(("gx", "gy")), P(), P("gx", "gy", None))
    )
    out_specs = (
        P(None, None, "gy", "gx"),
        field,
        field,
        P(("gx", "gy"), None),
        P("gx", "gy", None),
    )
    return jax.shard_map(
        per_device, mesh=mesh, in_specs=in_specs, out_specs=out_specs, check_vma=False
    )
```

time: 170 us -> 137 us (0.81); the launches traced: 168 us -> 137 us
  waiting for transfers between devices: 46.2 us -> 19.1 us
  local copies, waits for them, and re-layouts: 25.4 us -> 2.29 us
  blocking collectives: 0 us -> 21.1 us
  Pallas kernels: 44.7 us -> 57.8 us
  other arithmetic: 10.5 us -> 1.55 us
  starting transfers between devices: 37.9 us -> 34 us
  matrix products: 2.31 us -> 0 us
    all_to_all x3 -> x2, waiting for transfers between devices: 40.7 us -> 19.1 us  [the longest x1 16.7 us: per_device(): received = lax.all_to_all(send, ('gx', 'gy'), 0, 0, tiled=True)]
    all_to_all x0 -> x1, blocking collectives: none -> 21.1 us  [slip_response(): lax.all_to_all(sums.reshape(128, 8, 128), ('gx', 'gy'), 0, 0, tiled=True)]
    unnamed x30 -> x16, local copies, waits for them, and re-layouts: 15.5 us -> 0.77 us
    pallas_call x1 -> x5, Pallas kernels: 37 us -> 49.8 us  [the longest x1 32.4 us: four_steps(): pl.pallas_call(steps_kernel, out_shape=(jax.ShapeDtypeStruct((3, 8, 8, NY...]
    ppermute x6, waiting for transfers between devices: 5.57 us -> 0.02 us  [shifted(): return lax.ppermute(array, axis, pairs)]
    reduce_max x1 -> x0, other arithmetic: 4.6 us -> none  [slip_part(): target_of = jnp.max(jnp.where(matches, target[None, :], -1), axis=1)]
    all_to_all x2 -> x0, local copies, waits for them, and re-layouts: 3.88 us -> none  [slip_part(): lax.all_to_all(slip_weights, 'gy', split_axis=2, concat_axis=1, tiled=True)]
    concatenate x4, other arithmetic: 2.36 us -> 0.03 us  [phase_rows(): rows.append(jnp.concatenate([jnp.cos(angle), -jnp.sin(angle)]))]
  transfers between devices with their start and end apart: 9 -> 8, of which waited for: 5 -> 2; matrix products, arithmetic and copies ran while one was open for 13% -> 2% of each run, Pallas kernels for 0% -> 28%
where the time goes in v1:
time: 137 us
  Pallas kernels  57.8 us (42%)
  starting transfers between devices  34 us (25%)
  blocking collectives  21.1 us (15%)
  waiting for transfers between devices  19.1 us (14%)
  local copies, waits for them, and re-layouts  2.29 us (2%)
  other arithmetic  1.55 us (1%)
    pallas_call x1, Pallas kernels, four_steps(): pl.pallas_call(steps_kernel, out_shape=(jax.ShapeDtypeStruct((3, 8, 8, NY...  32.4 us
    all_to_all x1, blocking collectives, slip_response(): lax.all_to_all(sums.reshape(128, 8, 128), ('gx', 'gy'), 0, 0, tiled=True)  21.1 us
    all_to_all x1, waiting for transfers between devices, per_device(): received = lax.all_to_all(send, ('gx', 'gy'), 0, 0, tiled=True)  16.7 us
    ppermute x6, starting transfers between devices, shifted(): return lax.ppermute(array, axis, pairs)  15.9 us
    all_to_all x1, starting transfers between devices, per_device(): received = lax.all_to_all(send, ('gx', 'gy'), 0, 0, tiled=True)  12.1 us
    pallas_call x1, Pallas kernels, pack(): pl.pallas_call(pack_kernel, out_shape=(yshape, yshape, qshape), grid=(8,)...  8 us
    pallas_call x1, Pallas kernels, routed(): small_call(route_kernel, [(tiles, bf16), ((2, 128, 256), bf16), ((2, 128,...  6.33 us
    all_to_all x1, starting transfers between devices, per_device(): gathered = lax.all_to_all(message, 'gy', 0, 0, tiled=True)  6 us
  transfers between devices with their start and end apart: 8, of which 2 were waited for; matrix products, arithmetic and copies ran while one was open for 2% of the time, Pallas kernels for 28%

profile of v1, /device:TPU:1, one launch (start us, length us, event | category | flops | bytes accessed | tf_op | source)
XLA Modules:
  0.0 136.8 jit_solution(17612184438322719989)
XLA Ops:
  0.6 8.0 %pack.1 = (bf16[8,9,64,128]{3,2,1,0:T(8,128)(2,1)}, bf16[8,9,64,128]{3,2,1,0:T(8,128)(2,1)}, bf16[8,9,32,128]{3,2,1,0:T(8,128)(2,1)}) custom-call(f32[3,8,8,32,128]{4,3,2,1,0:T(8,128)} %bitcast.24, f32[8,8,32,128]{3,2,1,0:T(8,128)} %bitcast.26, f32[8,8,32,128]{3,2,1,0:T(8,128)} %bitcast.28, f32[8,8,32,128]{3,2,1,0:T(8,128)} %bitcast.30, ...), custom_call_target="tpu_custom_call" | custom-call | tf_op jit(solution)/shard_map/pack/pallas_call | solution.py:56
  8.6 4.9 %collective-permute-start.2 = (bf16[8,9,32,128]{3,2,1,0:T(8,128)(2,1)}, bf16[8,9,32,128]{3,2,1,0:T(8,128)(2,1)S(1)}, u32[]{:S(2)}, u32[]{:S(2)}) collective-permute-start(bf16[8,9,32,128]{3,2,1,0:T(8,128)(2,1)} %get-tuple-element.27), channel_id=1, source_target_pairs={{0,16},{16,32},{32,48},{48,64},{64,80},{80,96},{96,112},{1,17},{17... | collective-permute-start | bytes 1769480 | tf_op jit(solution)/shard_map/ppermute | solution.py:69
  13.6 1.9 %collective-permute-start.3 = (bf16[8,9,32,128]{3,2,1,0:T(8,128)(2,1)}, bf16[8,9,32,128]{3,2,1,0:T(8,128)(2,1)S(1)}, u32[]{:S(2)}, u32[]{:S(2)}) collective-permute-start(bf16[8,9,32,128]{3,2,1,0:T(8,128)(2,1)} %get-tuple-element.27), channel_id=1, source_target_pairs={{16,0},{32,16},{48,32},{64,48},{80,64},{96,80},{112,96},{17,1},{33... | collective-permute-start | bytes 1769480 | tf_op jit(solution)/shard_map/ppermute | solution.py:69
  15.5 3.2 %collective-permute-start = (bf16[8,9,64,128]{3,2,1,0:T(8,128)(2,1)}, bf16[8,9,64,128]{3,2,1,0:T(8,128)(2,1)S(1)}, u32[]{:S(2)}, u32[]{:S(2)}) collective-permute-start(bf16[8,9,64,128]{3,2,1,0:T(8,128)(2,1)} %get-tuple-element.25), channel_id=1, source_target_pairs={{0,1},{1,2},{2,3},{3,4},{4,5},{5,6},{6,7},{7,8},{8,9},{9,10},{10,1... | collective-permute-start | bytes 3538952 | tf_op jit(solution)/shard_map/ppermute | solution.py:69
  18.7 1.3 collective-permute-start.1
  20.0 0.6 pad_add_fusion.where
  20.6 6.3 %route.1 = (bf16[128,16,128]{2,1,0:T(8,128)(2,1)}, bf16[2,128,256]{2,1,0:T(8,128)(2,1)}, bf16[2,128,256]{2,1,0:T(8,128)(2,1)}, bf16[256,128]{1,0:T(8,128)(2,1)}, bf16[16,32,256]{2,1,0:T(8,128)(2,1)}) custom-call(s32[2]{0:T(128)} %pad_add_fusion.where, s32[64,512]{1,0:T(8,128)} %table.1, f32[256,256]{1,0:T(8,128)} %spectra.2, bf16[256,512]{1,0:T(8,128)(2,1)} %bitcast.40), custom_call_target="tpu_custom_call" | custom-call | tf_op jit(solution)/shard_map/route/pallas_call | solution.py:458
  27.0 12.1 %all-to-all-start = ((bf16[128,16,128]{2,1,0:T(8,128)(2,1)}), bf16[128,16,128]{2,1,0:T(8,128)(2,1)S(1)}, u32[]{:S(2)}, u32[]{:S(2)}) async-start(bf16[128,16,128]{2,1,0:T(8,128)(2,1)} %get-tuple-element.24), calls=%async_computation | async-start | bytes 1048576 | tf_op jit(solution)/shard_map/all_to_all | solution.py:514
  39.1 0.0 collective-permute-done.2
  39.1 0.0 collective-permute-done.3
  39.1 0.1 broadcast_select_fusion.side
  39.2 0.1 slice_bitcast_fusion
  39.3 3.3 %collective-permute-start.4 = (bf16[8,72,128]{2,1,0:T(8,128)(2,1)S(1)}, bf16[8,72,128]{2,1,0:T(8,128)(2,1)S(1)}, u32[]{:S(2)}, u32[]{:S(2)}) collective-permute-start(bf16[8,72,128]{2,1,0:T(8,128)(2,1)S(1)} %get-tuple-element.44), channel_id=1, source_target_pairs={{0,1},{1,2},{2,3},{3,4},{4,5},{5,6},{6,7},{7,8},{8,9},{9,10},{10,1... | collective-permute-start | bytes 442376 | tf_op jit(solution)/shard_map/ppermute | solution.py:69
  42.6 1.3 collective-permute-start.5
  43.9 16.7 %all-to-all-done.received = bf16[128,16,128]{2,1,0:T(8,128)(2,1)S(1)} async-done(((bf16[128,16,128]{2,1,0:T(8,128)(2,1)}), bf16[128,16,128]{2,1,0:T(8,128)(2,1)S(1)}, u32[]{:S(2)}, u32[]{:S(2)}) %all-to-all-start) | async-done | bytes 524320 | tf_op jit(solution)/shard_map/all_to_all | solution.py:514
  60.6 0.0 collective-permute-done.4.cprev
  60.6 0.0 collective-permute-done.5.cnext
  60.6 0.0 collective-permute-done.yprev
  60.6 0.0 collective-permute-done.1.ynext
  60.7 0.7 copy-done.2
  61.4 3.9 %sort.1 = (bf16[16,288,256]{2,1,0:T(8,128)(2,1)}, bf16[256,512]{1,0:T(8,128)(2,1)}) custom-call(bf16[128,16,128]{2,1,0:T(8,128)(2,1)} %copy-done.2, bf16[2,128,256]{2,1,0:T(8,128)(2,1)} %get-tuple-element.29.place, bf16[2,128,256]{2,1,0:T(8,128)(2,1)} %get-tuple-element.30.pick, bf16[16,32,256]{2,1,0:T(8,128)(2,1)} %get-tuple-element.31.turned), custom_call_target="tpu_custom_call" | custom-call | tf_op jit(solution)/shard_map/sort/pallas_call | solution.py:475
  65.3 0.0 copy-done.5
  65.3 0.0 copy-done.3
  65.3 6.0 %all-to-all-start.1 = ((bf16[16,288,256]{2,1,0:T(8,128)(2,1)}), bf16[16,288,256]{2,1,0:T(8,128)(2,1)S(1)}, u32[]{:S(2)}, u32[]{:S(2)}) async-start(bf16[16,288,256]{2,1,0:T(8,128)(2,1)} %get-tuple-element.32), calls=%async_computation.1 | async-start | bytes 4718592 | tf_op jit(solution)/shard_map/all_to_all | solution.py:517
  71.3 0.8 copy.16.lane_of
  72.4 0.6 pad_maximum_fusion.phase
  73.0 32.4 %four_steps.1 = (f32[3,8,8,32,128]{4,3,2,1,0:T(8,128)}, f32[8,8,32,128]{3,2,1,0:T(8,128)}, f32[8,8,32,128]{3,2,1,0:T(8,128)}, f32[256,256]{1,0:T(8,128)}, f32[256,128]{1,0:T(8,128)}) custom-call(s32[256]{0:T(256)} %cell.1, f32[3,8,8,32,128]{4,3,2,1,0:T(8,128)} %bitcast.25, f32[8,8,32,128]{3,2,1,0:T(8,128)} %bitcast.27, f32[8,8,32,128]{3,2,1,0:T(8,128)} %bitcast.29, ...), custom_call_target="tpu_custom_call" | custom-call | tf_op jit(solution)/shard_map/four_steps/pallas_call | solution.py:261
  105.4 2.4 %all-to-all-done.1.gathered = bf16[16,288,256]{2,1,0:T(8,128)(2,1)S(1)} async-done(((bf16[16,288,256]{2,1,0:T(8,128)(2,1)}), bf16[16,288,256]{2,1,0:T(8,128)(2,1)S(1)}, u32[]{:S(2)}, u32[]{:S(2)}) %all-to-all-start.1) | async-done | bytes 2359328 | tf_op jit(solution)/shard_map/all_to_all | solution.py:517
  107.8 3.7 %sums.1 = f32[8,16,8,128]{3,2,1,0:T(8,128)} custom-call(f32[256,128]{1,0:T(8,128)} %get-tuple-element.40.samples, bf16[256,128]{1,0:T(8,128)(2,1)} %get-tuple-element.41.hot, bf16[256,512]{1,0:T(8,128)(2,1)} %get-tuple-element.42.patch_weights), custom_call_target="tpu_custom_call" | custom-call | tf_op jit(solution)/shard_map/sums/pallas_call | solution.py:487
  111.4 21.1 %all_to_all.15.sums = f32[128,8,128]{2,1,0:T(8,128)} all-to-all(f32[128,8,128]{2,1,0:T(8,128)} %bitcast.38), channel_id=1, replica_groups=mesh['gx'=8,'gy'=16] {'gx','gy'}, dimensions={0} | all-to-all | bytes 1048576 | tf_op jit(solution)/shard_map/all_to_all | solution.py:490
  132.5 0.7 broadcast_in_dim.12
  133.2 3.6 %slip.1 = f32[8,32,256]{2,1,0:T(8,128)} custom-call(bf16[16,288,256]{2,1,0:T(8,128)(2,1)} %copy-done, f32[128,8,128]{2,1,0:T(8,128)} %all_to_all.15.sums, f32[128,256]{1,0:T(8,128)} %bitcast.39), custom_call_target="tpu_custom_call" | custom-call | tf_op jit(solution)/shard_map/slip/pallas_call | solution.py:492
  (23 shorter events, 0.3 us)
Async XLA Ops:
  8.6 30.5 %collective-permute-start.2 = (bf16[8,9,32,128]{3,2,1,0:T(8,128)(2,1)}, bf16[8,9,32,128]{3,2,1,0:T(8,128)(2,1)S(1)}, u32[]{:S(2)}, u32[]{:S(2)}) collective-permute-start(bf16[8,9,32,128]{3,2,1,0:T(8,128)(2,1)} %get-tuple-element.27), channel_id=1, source_target_pairs={{0,16},{16,32},{32,48},{48,64},{64,80},{80,96},{96,112},{1,17},{17... | collective-permute-start | bytes 1769480 | tf_op jit(solution)/shard_map/ppermute | solution.py:69
  13.6 25.6 %collective-permute-start.3 = (bf16[8,9,32,128]{3,2,1,0:T(8,128)(2,1)}, bf16[8,9,32,128]{3,2,1,0:T(8,128)(2,1)S(1)}, u32[]{:S(2)}, u32[]{:S(2)}) collective-permute-start(bf16[8,9,32,128]{3,2,1,0:T(8,128)(2,1)} %get-tuple-element.27), channel_id=1, source_target_pairs={{16,0},{32,16},{48,32},{64,48},{80,64},{96,80},{112,96},{17,1},{33... | collective-permute-start | bytes 1769480 | tf_op jit(solution)/shard_map/ppermute | solution.py:69
  15.5 45.1 %collective-permute-start = (bf16[8,9,64,128]{3,2,1,0:T(8,128)(2,1)}, bf16[8,9,64,128]{3,2,1,0:T(8,128)(2,1)S(1)}, u32[]{:S(2)}, u32[]{:S(2)}) collective-permute-start(bf16[8,9,64,128]{3,2,1,0:T(8,128)(2,1)} %get-tuple-element.25), channel_id=1, source_target_pairs={{0,1},{1,2},{2,3},{3,4},{4,5},{5,6},{6,7},{7,8},{8,9},{9,10},{10,1... | collective-permute-start | bytes 3538952 | tf_op jit(solution)/shard_map/ppermute | solution.py:69
  18.7 42.0 %collective-permute-start.1 = (bf16[8,9,64,128]{3,2,1,0:T(8,128)(2,1)}, bf16[8,9,64,128]{3,2,1,0:T(8,128)(2,1)}, u32[]{:S(2)}, u32[]{:S(2)}) collective-permute-start(bf16[8,9,64,128]{3,2,1,0:T(8,128)(2,1)} %get-tuple-element.26), channel_id=1, source_target_pairs={{1,0},{2,1},{3,2},{4,3},{5,4},{6,5},{7,6},{8,7},{9,8},{10,9},{11,1... | collective-permute-start | bytes 3538952 | tf_op jit(solution)/shard_map/ppermute | solution.py:69
  27.0 33.6 %all-to-all-start = ((bf16[128,16,128]{2,1,0:T(8,128)(2,1)}), bf16[128,16,128]{2,1,0:T(8,128)(2,1)S(1)}, u32[]{:S(2)}, u32[]{:S(2)}) async-start(bf16[128,16,128]{2,1,0:T(8,128)(2,1)} %get-tuple-element.24), calls=%async_computation | async-start | bytes 1048576 | tf_op jit(solution)/shard_map/all_to_all | solution.py:514
  39.2 26.1 %copy-start.1 = (bf16[8,9,32,128]{3,2,1,0:T(8,128)(2,1)}, bf16[8,9,32,128]{3,2,1,0:T(8,128)(2,1)S(1)}, u32[]{:S(2)}) copy-start(bf16[8,9,32,128]{3,2,1,0:T(8,128)(2,1)S(1)} %broadcast_select_fusion.side) | copy-start | bytes 1769476
  39.3 21.3 %collective-permute-start.4 = (bf16[8,72,128]{2,1,0:T(8,128)(2,1)S(1)}, bf16[8,72,128]{2,1,0:T(8,128)(2,1)S(1)}, u32[]{:S(2)}, u32[]{:S(2)}) collective-permute-start(bf16[8,72,128]{2,1,0:T(8,128)(2,1)S(1)} %get-tuple-element.44), channel_id=1, source_target_pairs={{0,1},{1,2},{2,3},{3,4},{4,5},{5,6},{6,7},{7,8},{8,9},{9,10},{10,1... | collective-permute-start | bytes 442376 | tf_op jit(solution)/shard_map/ppermute | solution.py:69
  42.6 18.0 %collective-permute-start.5 = (bf16[8,72,128]{2,1,0:T(8,128)(2,1)S(1)}, bf16[8,72,128]{2,1,0:T(8,128)(2,1)S(1)}, u32[]{:S(2)}, u32[]{:S(2)}) collective-permute-start(bf16[8,72,128]{2,1,0:T(8,128)(2,1)S(1)} %get-tuple-element.43), channel_id=1, source_target_pairs={{1,0},{2,1},{3,2},{4,3},{5,4},{6,5},{7,6},{8,7},{9,8},{10,9},{11,1... | collective-permute-start | bytes 442376 | tf_op jit(solution)/shard_map/ppermute | solution.py:69
  60.6 0.8 copy-start.2
  60.6 4.7 %copy-start.4 = (bf16[8,72,128]{2,1,0:T(8,128)(2,1)}, bf16[8,72,128]{2,1,0:T(8,128)(2,1)S(1)}, u32[]{:S(2)}) copy-start(bf16[8,72,128]{2,1,0:T(8,128)(2,1)S(1)} %collective-permute-done.4.cprev) | copy-start | bytes 442372
  60.6 4.7 %copy-start.5 = (bf16[8,72,128]{2,1,0:T(8,128)(2,1)}, bf16[8,72,128]{2,1,0:T(8,128)(2,1)S(1)}, u32[]{:S(2)}) copy-start(bf16[8,72,128]{2,1,0:T(8,128)(2,1)S(1)} %collective-permute-done.5.cnext) | copy-start | bytes 442372
  60.6 4.7 %copy-start.3 = (bf16[8,9,64,128]{3,2,1,0:T(8,128)(2,1)}, bf16[8,9,64,128]{3,2,1,0:T(8,128)(2,1)S(1)}, u32[]{:S(2)}) copy-start(bf16[8,9,64,128]{3,2,1,0:T(8,128)(2,1)S(1)} %collective-permute-done.yprev) | copy-start | bytes 3538948
  65.3 6.0 %copy-start.7 = (s32[256]{0:T(256)S(1)}, s32[256]{0:T(256)}, u32[]{:S(2)}) copy-start(s32[256]{0:T(256)} %cell.1) | copy-start | bytes 3076
  65.3 42.5 %all-to-all-start.1 = ((bf16[16,288,256]{2,1,0:T(8,128)(2,1)}), bf16[16,288,256]{2,1,0:T(8,128)(2,1)S(1)}, u32[]{:S(2)}, u32[]{:S(2)}) async-start(bf16[16,288,256]{2,1,0:T(8,128)(2,1)} %get-tuple-element.32), calls=%async_computation.1 | async-start | bytes 4718592 | tf_op jit(solution)/shard_map/all_to_all | solution.py:517
  73.0 59.5 %copy-start.6 = (f32[4,256]{1,0:T(4,128)S(1)}, f32[4,256]{1,0:T(4,128)}, u32[]{:S(2)}) copy-start(f32[4,256]{1,0:T(4,128)} %pad_maximum_fusion.phase) | copy-start | bytes 12292
  107.8 25.4 %copy-start = (bf16[16,288,256]{2,1,0:T(8,128)(2,1)}, bf16[16,288,256]{2,1,0:T(8,128)(2,1)S(1)}, u32[]{:S(2)}) copy-start(bf16[16,288,256]{2,1,0:T(8,128)(2,1)S(1)} %all-to-all-done.1.gathered) | copy-start | bytes 7077892

commit v2 on v1

--- a/solution.py
+++ b/solution.py
@@ -1,7 +1,6 @@
-import functools
-
 import jax
 import jax.numpy as jnp
+import numpy as np
 from jax import lax
 from jax.experimental import pallas as pl
 from jax.experimental.pallas import tpu as pltpu
@@ -15,6 +14,9 @@
 FIELDS = 9
 VX, VY, VZ, PR, ME, BU, MO, RE, ST = range(FIELDS)
 BP = FIELDS
+REACH = [7, 7, 6, 8, 6, 7, 6, 6, 6]
+SENT = [(f, d) for f in range(FIELDS) for d in range(REACH[f])]
+ROWS = 8 * (len(SENT) + len(SENT) % 2)
 
 
 def lanes(shape):
@@ -26,32 +28,37 @@
     return pltpu.roll(x, shift, axis) if shift else x
 
 
-def pack_kernel(vel, pr, me, bu, mo, re, st, lo_ref, hi_ref, q_ref):
+def pack_kernel(vel, pr, me, bu, mo, re, st, lo_ref, hi_ref, q_ref, lows, highs):
     lane = lanes((NY, 128))
     fields = [vel.at[0], vel.at[1], vel.at[2], pr, me, bu, mo, re, st]
     for f, ref in enumerate(fields):
-        lows, highs = [], []
         strip = jnp.zeros((NY, 128), jnp.float32)
         for g in range(8):
-            plane = ref[g, 0]
-            turned = roll(plane, 8 + 16 * g)
+            turned = roll(ref[g, 0], 8 + 16 * g)
             strip = jnp.where((lane >> 4) == g, turned, strip)
-            ends = turned[:HALO], turned[NY - HALO :]
+            low, high = turned[:HALO], turned[NY - HALO :]
             if f == VX:
-                ends = tuple(roll(e, -1) for e in ends)
-            lows.append(ends[0])
-            highs.append(ends[1])
-        lo_ref[0, f] = jnp.concatenate(lows, axis=0).astype(jnp.bfloat16)
-        hi_ref[0, f] = jnp.concatenate(highs, axis=0).astype(jnp.bfloat16)
+                low, high = roll(low, -1), roll(high, -1)
+            lows[f, pl.ds(8 * g, 8)] = low
+            highs[f, pl.ds(8 * g, 8)] = high
         q_ref[0, f] = strip.astype(jnp.bfloat16)
+    for ref, ends, first in ((lo_ref, lows, False), (hi_ref, highs, True)):
+        tiles = [
+            ends[f, pl.ds(d + (HALO - REACH[f] if first else 0), 8, stride=8)] for f, d in SENT
+        ]
+        if len(tiles) % 2:
+            tiles.append(tiles[-1])
+        for t in range(0, len(tiles), 2):
+            pair = jnp.concatenate(tiles[t : t + 2], axis=0)
+            ref[0, pl.ds(8 * t, 16)] = pair.astype(jnp.bfloat16)
 
 
 def pack(velocity, *fields):
     spec = pl.BlockSpec((8, 1, NY, NX), lambda i: (0, i, 0, 0))
     vspec = pl.BlockSpec((3, 8, 1, NY, NX), lambda i: (0, 0, i, 0, 0))
-    yspec = pl.BlockSpec((1, FIELDS, 64, 128), lambda i: (i, 0, 0, 0))
+    yspec = pl.BlockSpec((1, ROWS, 128), lambda i: (i, 0, 0))
     qspec = pl.BlockSpec((1, FIELDS, NY, 128), lambda i: (i, 0, 0, 0))
-    yshape = jax.ShapeDtypeStruct((8, FIELDS, 64, 128), jnp.bfloat16)
+    yshape = jax.ShapeDtypeStruct((8, ROWS, 128), jnp.bfloat16)
     qshape = jax.ShapeDtypeStruct((8, FIELDS, NY, 128), jnp.bfloat16)
     return pl.pallas_call(
         pack_kernel,
@@ -59,6 +66,7 @@
         grid=(8,),
         in_specs=[vspec] + [spec] * 6,
         out_specs=(yspec, yspec, qspec),
+        scratch_shapes=[pltpu.VMEM((FIELDS, 64, 128), jnp.float32)] * 2,
         name="pack",
     )(velocity.reshape(3, 8, 8, NY, NX), *[f.reshape(8, 8, NY, NX) for f in fields])
 
@@ -92,7 +100,8 @@
     st,
     spectra,
     phase,
-    lane_of,
+    hot,
+    patch_weights,
     yprev,
     ynext,
     side,
@@ -102,12 +111,14 @@
     pr_o,
     me_o,
     spec_o,
-    samp_o,
+    sums_o,
     E,
     S,
     X,
+    T,
     shear,
     G,
+    L,
     sems,
 ):
     sources = [vel.at[0], vel.at[1], vel.at[2], pr, me, bu, mo, re, st]
@@ -126,12 +137,16 @@
     def fill(zi):
         cp = cprev[zi].astype(jnp.float32)
         cn = cnext[zi].astype(jnp.float32)
+        for ref, ends, first in ((ynext, T.at[0], False), (yprev, T.at[1], True)):
+            for t in range(0, len(SENT), 2):
+                pair = ref[zi, pl.ds(8 * t, 16)].astype(jnp.float32)
+                for k, (f, d) in enumerate(SENT[t : t + 2]):
+                    at = d + (HALO - REACH[f] if first else 0)
+                    ends[f, pl.ds(at, 8, stride=8)] = pair[8 * k : 8 * k + 8]
         for f in range(FIELDS):
-            yp = yprev[zi, f].astype(jnp.float32)
-            yn = ynext[zi, f].astype(jnp.float32)
             for g in range(8):
                 z = g * 10 + zi + 1
-                low, high = yp[8 * g : 8 * g + 8], yn[8 * g : 8 * g + 8]
+                low, high = T[1, f, pl.ds(8 * g, 8)], T[0, f, pl.ds(8 * g, 8)]
                 mid = roll(X[f, g, zi], (7 if f == VX else 8) + 16 * g)
                 E[f, z, :HALO] = low
                 E[f, z, HALO + NY :] = high
@@ -159,8 +174,7 @@
             E[f, 10 * g] = roll(E[f, 10 * g - 2], 16) if g else zero
             E[f, 10 * g + 9] = roll(E[f, 10 * g + 11], -16) if g < 7 else zero
 
-    spec_o[...] = spectra[...]
-    samp_o[...] = jnp.zeros_like(samp_o)
+    T[...] = jnp.zeros_like(T)
     for zi in range(8):
         for c in copies[zi]:
             c.wait()
@@ -173,7 +187,7 @@
         ref[VY, z] = ref[VY, z] - b * ydiff(p)
         ref[VZ, z] = ref[VZ, z] - b * (ref[PR, z + 1] - ref[PR, z - 1])
 
-    def velocities(zi, _):
+    def velocities(zi):
         zs = zi + 1
         ps = S[PR, zs]
         join = zero
@@ -183,16 +197,16 @@
             moved(E, z, turned_diff(p, ps, lane - 16 * g), p)
             join = jnp.where(group == g, p, join)
         moved(S, zs, turned_diff(ps, join, lane16), ps)
-        return 0
-
-    def updated(ref, z, spread):
-        m = ref[ME, z]
-        m = m - ref[RE, z] * (m + ref[ST, z] * spread)
-        ref[ME, z] = m
-        ref[PR, z] = ref[PR, z] - ref[MO, z] * (spread + m)
-
-    def pressures(zi, _):
+
+    def updated(ref, z, spread, rows):
+        m = ref[ME, z, rows]
+        m = m - ref[RE, z, rows] * (m + ref[ST, z, rows] * spread)
+        ref[ME, z, rows] = m
+        ref[PR, z, rows] = ref[PR, z, rows] - ref[MO, z, rows] * (spread + m)
+
+    def pressures(n, last, zi):
         zs = zi + 1
+        rows = slice(HALO, HALO + NY) if last else slice(0, EY)
         svx, svy = S[VX, zs], S[VY, zs]
         svy_in = svy[HALO : HALO + NY]
         lane_in = lane[:NY]
@@ -200,38 +214,35 @@
         for g in range(8):
             z = g * 10 + zi + 1
             vx, vy = E[VX, z], E[VY, z]
-            spread = back_diff(vx, svx, lane - 16 * g) + ydiff(vy)
-            updated(E, z, spread + (E[VZ, z + 1] - E[VZ, z - 1]))
-            row = pl.multiple_of((g * 8 + zi) * NY, NY)
+            spread = back_diff(vx[rows], svx[rows], lane[rows] - 16 * g) + ydiff(vy)[rows]
+            updated(E, z, spread + (E[VZ, z + 1, rows] - E[VZ, z - 1, rows]), rows)
+            row = pl.multiple_of((n * NZ + g * 8 + zi) * NY, NY)
             shear[pl.ds(row, NY), :] = ydiff(vx)[HALO : HALO + NY] + turned_diff(
                 vy[HALO : HALO + NY], svy_in, lane_in - 16 * g
             )
-            join = jnp.where(group == g, vx, join)
-        spread = back_diff(svx, join, lane16) + ydiff(svy)
-        updated(S, zs, spread + (S[VZ, zs + 1] - S[VZ, zs - 1]))
+            if not last:
+                join = jnp.where(group == g, vx, join)
+        if not last:
+            spread = back_diff(svx, join, lane16) + ydiff(svy)
+            updated(S, zs, spread + (S[VZ, zs + 1] - S[VZ, zs - 1]), rows)
+
+    def looped(body):
+        def one(zi, _):
+            body(zi)
+            return 0
+
+        lax.fori_loop(0, 8, one, 0)
+
+    def step(n, last):
+        looped(velocities)
+        wrap_planes(VZ)
+        looped(lambda zi: pressures(n, last, zi))
+        if not last:
+            wrap_planes(PR)
         return 0
 
-    wanted = lanes((256, 128)) == lane_of[...]
-
-    def step(n, _):
-        lax.fori_loop(0, 8, velocities, 0)
-        wrap_planes(VZ)
-        lax.fori_loop(0, 8, pressures, 0)
-        wrap_planes(PR)
-
-        def pick(i, _):
-            for k in range(8):
-                c = cell[i * 8 + k]
-                G[pl.ds(i * 8 + k, 1), :] = shear[pl.ds(c >> 7, 1), :]
-            return 0
-
-        lax.fori_loop(0, 32, pick, 0)
-        sample = jnp.sum(jnp.where(wanted, G[...], 0.0), axis=1, keepdims=True)
-        spec_o[...] = spec_o[...] + sample * phase[pl.ds(n, 1), :]
-        samp_o[...] = jnp.where(lanes((256, 128)) == n, sample, samp_o[...])
-        return 0
-
-    lax.fori_loop(0, STEPS, step, 0)
+    lax.fori_loop(0, STEPS - 1, lambda n, _: step(n, False), 0)
+    step(STEPS - 1, True)
     targets = [vel_o.at[0], vel_o.at[1], vel_o.at[2], pr_o, me_o]
     outs = []
     for zi in range(8):
@@ -241,40 +252,70 @@
                 X[f, g, zi] = roll(plane, -(7 if f == VX else 8) - 16 * g)
             outs.append(pltpu.make_async_copy(X.at[f, :, zi], dst.at[:, zi], sems.at[f, zi]))
             outs[-1].start()
+
+    def pick(i, _):
+        for k in range(8):
+            at = i * 8 + k
+            c = cell[at]
+            for n in range(STEPS):
+                G[n, pl.ds(at, 1), :] = shear[pl.ds(n * NZ * NY + (c >> 7), 1), :]
+            L[pl.ds(at, 1), :] = jnp.full((1, 128), (c + 7 + 16 * (c >> 15)) & 127, jnp.int32)
+        return 0
+
+    lax.fori_loop(0, 32, pick, 0)
+    wanted = lanes((256, 128)) == L[...]
+    listed = hot[...].astype(jnp.float32)
+    spec = spectra[...]
+    sums = []
+    for n in range(STEPS):
+        sample = jnp.sum(jnp.where(wanted, G[n], 0.0), axis=1, keepdims=True)
+        spec = spec + sample * phase[n : n + 1, :]
+        scaled = listed * sample
+        high = scaled.astype(jnp.bfloat16).astype(jnp.float32)
+        both = high + roll(scaled - high, 64)
+        total = transposed_dot(both.astype(jnp.bfloat16), patch_weights[...])
+        sums.append(total[:64] + total[64:])
+    spec_o[...] = spec
+    quarter = lanes((64, 128)) >> 5
+    for j in range(16):
+        block = slice(128 * (j // 4), 128 * (j // 4) + 128)
+        packed = jnp.zeros((64, 128), jnp.float32)
+        for n in range(STEPS):
+            packed = jnp.where(quarter == n, roll(sums[n][:, block], 32 * (n - j % 4)), packed)
+        sums_o[:, j] = packed.reshape(8, 8, 128)
     for c in outs:
         c.wait()
 
 
 def phase_rows(freqs):
-    rows = []
-    for step in range(1, STEPS + 1):
-        angle = jnp.pi * (jnp.arange(freqs, dtype=jnp.float32) + 0.5) / freqs * step
-        rows.append(jnp.concatenate([jnp.cos(angle), -jnp.sin(angle)]))
-    return jnp.stack(rows)
-
-
-def four_steps(velocity, fields, spectra, patch_cell, halos):
+    angle = np.pi * (np.arange(freqs) + 0.5) / freqs * np.arange(1, STEPS + 1)[:, None]
+    return np.concatenate([np.cos(angle), -np.sin(angle)], axis=1).astype(np.float32)
+
+
+def four_steps(velocity, fields, spectra, patch_cell, hot, patch_weights, halos):
     any_spec = pl.BlockSpec(memory_space=pl.ANY)
     vmem = pl.BlockSpec(memory_space=pltpu.VMEM)
     smem = pl.BlockSpec(memory_space=pltpu.SMEM)
     field = jax.ShapeDtypeStruct((8, 8, NY, NX), jnp.float32)
-    vel, pr, me, spec, samples = pl.pallas_call(
+    vel, pr, me, spec, sums = pl.pallas_call(
         steps_kernel,
         out_shape=(
             jax.ShapeDtypeStruct((3, 8, 8, NY, NX), jnp.float32),
             field,
             field,
             jax.ShapeDtypeStruct(spectra.shape, jnp.float32),
-            jax.ShapeDtypeStruct((spectra.shape[0], 128), jnp.float32),
+            jax.ShapeDtypeStruct((8, 16, 8, 128), jnp.float32),
         ),
-        in_specs=[smem] + [any_spec] * 7 + [vmem] * 8,
+        in_specs=[smem] + [any_spec] * 7 + [vmem] * 9,
         out_specs=(any_spec, any_spec, any_spec, vmem, vmem),
         scratch_shapes=[
             pltpu.VMEM((FIELDS + 1, 80, EY, 128), jnp.float32),
             pltpu.VMEM((FIELDS + 1, 10, EY, 128), jnp.float32),
             pltpu.VMEM((FIELDS, 8, 8, NY, 128), jnp.float32),
-            pltpu.VMEM((NZ * NY, 128), jnp.float32),
-            pltpu.VMEM((256, 128), jnp.float32),
+            pltpu.VMEM((2, FIELDS, 64, 128), jnp.float32),
+            pltpu.VMEM((STEPS * NZ * NY, 128), jnp.float32),
+            pltpu.VMEM((STEPS, 256, 128), jnp.float32),
+            pltpu.VMEM((256, 128), jnp.int32),
             pltpu.SemaphoreType.DMA((FIELDS, 8)),
         ],
         compiler_params=pltpu.CompilerParams(vmem_limit_bytes=56 * 1024 * 1024),
@@ -284,12 +325,28 @@
         velocity.reshape(3, 8, 8, NY, NX),
         *[f.reshape(8, 8, NY, NX) for f in fields],
         spectra,
-        phase_rows(spectra.shape[1] // 2),
-        ((patch_cell + 7 + 16 * (patch_cell >> 15)) & 127)[:, None],
+        jnp.asarray(phase_rows(spectra.shape[1] // 2)),
+        hot,
+        patch_weights,
         *halos,
     )
     shape = (NZ, NY, NX)
-    return vel.reshape(velocity.shape), pr.reshape(shape), me.reshape(shape), spec, samples
+    return vel.reshape(velocity.shape), pr.reshape(shape), me.reshape(shape), spec, sums
+
+
+def join_kernel(left, right, side, low, high):
+    from_left = (lanes((NY, 128)) & 15) < 8
+    for zi in range(8):
+        lows, highs = [], []
+        for f in range(FIELDS):
+            strip = jnp.where(
+                from_left, left[zi, f].astype(jnp.float32), right[zi, f].astype(jnp.float32)
+            )
+            side[zi, f] = strip.astype(jnp.bfloat16)
+            lows.append(strip[:HALO])
+            highs.append(strip[NY - HALO :])
+        low[zi] = jnp.concatenate(lows, axis=0).astype(jnp.bfloat16)
+        high[zi] = jnp.concatenate(highs, axis=0).astype(jnp.bfloat16)
 
 
 def halo_exchange(velocity, fields):
@@ -298,9 +355,16 @@
     ynext = shifted(lo, "gy", False)
     left = shifted(q, "gx", True)
     right = shifted(q, "gx", False)
-    side = jnp.where((jnp.arange(128) & 15) < 8, left, right)
-    cprev = shifted(side[:, :, NY - HALO :].reshape(8, FIELDS * HALO, 128), "gy", True)
-    cnext = shifted(side[:, :, :HALO].reshape(8, FIELDS * HALO, 128), "gy", False)
+    side, low, high = small_call(
+        join_kernel,
+        [(q.shape, jnp.bfloat16)] + [((8, FIELDS * HALO, 128), jnp.bfloat16)] * 2,
+        "join",
+        (),
+        0,
+        2,
+    )(left, right)
+    cprev = shifted(high, "gy", True)
+    cnext = shifted(low, "gy", False)
     return yprev, ynext, side, cprev, cnext
 
 
@@ -322,9 +386,9 @@
     return jnp.sum(jnp.where(eye, row, 0.0), axis=1, keepdims=True)
 
 
-def route_kernel(where, table, spectra, weights, send, place, pick, hot, turned, stage):
+def route_kernel(table, spectra, weights, send, place, pick, hot, turned, stage):
     n = spectra.shape[0]
-    gx, gy = where[0], where[1]
+    gx, gy = lax.axis_index("gx"), lax.axis_index("gy")
     base = (gx * 16 + gy) * n
     mine = table[pl.ds(pl.multiple_of(gx * 8, 8), 8), :].astype(jnp.float32)
     mine = pltpu.roll(mine, lax.rem(512 - 32 * gy, 512), 1)[:, :128]
@@ -398,43 +462,27 @@
         message[j, 256:] = turned[j]
 
 
-def sums_kernel(samples, hot, patch_weights, out):
-    lane = lanes((256, 128))
-    sums = []
-    listed = hot[...].astype(jnp.float32)
-    for n in range(STEPS):
-        sample = jnp.sum(jnp.where(lane == n, samples[...], 0.0), axis=1, keepdims=True)
-        scaled = listed * sample
-        high = scaled.astype(jnp.bfloat16)
-        rest = (scaled - high.astype(jnp.float32)).astype(jnp.bfloat16).astype(jnp.float32)
-        both = scaled.astype(jnp.bfloat16).astype(jnp.float32) + roll(rest, 64)
-        total = transposed_dot(both.astype(jnp.bfloat16), patch_weights[...])
-        sums.append(total[:64] + total[64:])
-    quarter = lanes((64, 128)) >> 5
+def product_kernel(gathered, out):
+    square = (256, 256)
+    same = ((rows_of(square) >> 5) == (lanes(square) >> 5)).astype(jnp.float32)
+    same = same.astype(jnp.bfloat16)
+    total = jnp.zeros(square, jnp.float32)
     for j in range(16):
-        block = slice(128 * (j // 4), 128 * (j // 4) + 128)
-        packed = jnp.zeros((64, 128), jnp.float32)
-        for n in range(STEPS):
-            packed = jnp.where(quarter == n, roll(sums[n][:, block], 32 * (n - j % 4)), packed)
-        out[:, j] = packed.reshape(8, 8, 128)
-
-
-def slip_kernel(gathered, sums, phase, out):
+        spread = jnp.concatenate([gathered[j, 256:]] * 8, axis=0) * same
+        total += jnp.dot(spread, gathered[j, :256], preferred_element_type=jnp.float32)
+    out[...] = total
+
+
+def slip_kernel(product, sums, phase, out):
     total = jnp.sum(sums[...], axis=0)
     own = (lanes((32, 128)) & 31) == rows_of((32, 128))
     left = jnp.concatenate(
         [jnp.where(own, total[r : r + 1], 0.0) for r in range(8)], axis=0
     )
-    slip = jnp.dot(
+    added = jnp.dot(
         left, phase[...], precision=lax.Precision.HIGHEST, preferred_element_type=jnp.float32
     )
-    square = (256, 256)
-    same = ((rows_of(square) >> 5) == (lanes(square) >> 5)).astype(jnp.float32)
-    same = same.astype(jnp.bfloat16)
-    for j in range(16):
-        spread = jnp.concatenate([gathered[j, 256:]] * 8, axis=0) * same
-        slip += jnp.dot(spread, gathered[j, :256], preferred_element_type=jnp.float32)
-    out[...] = slip.reshape(out.shape)
+    out[...] = (product[...] + added).reshape(out.shape)
 
 
 def small_call(kernel, outs, name, scratch=(), smem=0, inputs=0):
@@ -453,7 +501,6 @@
 
 def routed(spectra, rupture_patches, slip_weights):
     bf16, f32 = jnp.bfloat16, jnp.float32
-    where = jnp.stack([lax.axis_index("gx"), lax.axis_index("gy")])
     tiles = (128, 16, 128)
     return small_call(
         route_kernel,
@@ -466,9 +513,9 @@
         ],
         "route",
         [pltpu.VMEM(tiles, f32)],
-        1,
-        4,
-    )(where, rupture_patches, spectra, slip_weights.reshape(256, 512))
+        0,
+        3,
+    )(rupture_patches, spectra, slip_weights.reshape(256, 512))
 
 
 def sorted_rows(received, place, pick, turned):
@@ -482,15 +529,14 @@
     )(received, place, pick, turned)
 
 
-def slip_response(gathered, patch_weights, hot, samples):
+def slip_response(gathered, sums):
     f32 = jnp.float32
-    (sums,) = small_call(sums_kernel, [((8, 16, 8, 128), f32)], "sums", (), 0, 3)(
-        samples, hot, patch_weights
-    )
+    sums, gathered = lax.optimization_barrier((sums, gathered))
     sums = lax.all_to_all(sums.reshape(128, 8, 128), ("gx", "gy"), 0, 0, tiled=True)
-    phase = jnp.repeat(phase_rows(128), 32, axis=0)
+    (product,) = small_call(product_kernel, [((256, 256), f32)], "product", (), 0, 1)(gathered)
+    phase = jnp.asarray(np.repeat(phase_rows(128), 32, axis=0))
     (slip,) = small_call(slip_kernel, [((8, 32, 256), f32)], "slip", (), 0, 3)(
-        gathered, sums, phase
+        product, sums, phase
     )
     return slip
 
@@ -516,11 +562,10 @@
     message, patch_weights = sorted_rows(received, place, pick, turned)
     gathered = lax.all_to_all(message, "gy", 0, 0, tiled=True)
     spectra, message = lax.optimization_barrier((spectra, message))
-    velocity, pressure, memory, spectra, samples = four_steps(
-        velocity, fields, spectra, patch_cell, halos
-    )
-    samples, gathered = lax.optimization_barrier((samples, gathered))
-    slip = slip_response(gathered, patch_weights, hot, samples)
+    velocity, pressure, memory, spectra, sums = four_steps(
+        velocity, fields, spectra, patch_cell, hot, patch_weights, halos
+    )
+    slip = slip_response(gathered, sums)
     return (velocity, pressure, memory, spectra, slip)
 
 

time: 137 us -> 124 us (0.905)
  blocking collectives: 21.1 us -> 0 us
  starting transfers between devices: 34 us -> 44.5 us
  other arithmetic: 1.55 us -> 0 us
    all_to_all x1 -> x0, blocking collectives: 21.1 us -> none  [slip_response(): lax.all_to_all(sums.reshape(128, 8, 128), ('gx', 'gy'), 0, 0, tiled=True)]
    all_to_all x0 -> x1, waiting for transfers between devices: none -> 10.8 us  [slip_response(): lax.all_to_all(sums.reshape(128, 8, 128), ('gx', 'gy'), 0, 0, tiled=True)]
    all_to_all x0 -> x1, starting transfers between devices: none -> 10.6 us  [slip_response(): lax.all_to_all(sums.reshape(128, 8, 128), ('gx', 'gy'), 0, 0, tiled=True)]
    all_to_all x1, waiting for transfers between devices: 16.7 us -> 6.23 us  [per_device(): received = lax.all_to_all(send, ('gx', 'gy'), 0, 0, tiled=True)]
    unnamed x16, local copies, waits for them, and re-layouts: 0.77 us -> 2.75 us
    pallas_call x1 -> x2, Pallas kernels: 3.66 us -> 5.33 us  [the longest x1 3.08 us: slip_response(): small_call(product_kernel, [((256, 256), f32)], 'product', (), 0, 1)]
    all_to_all x1, waiting for transfers between devices: 2.38 us -> 0.85 us  [per_device(): gathered = lax.all_to_all(message, 'gy', 0, 0, tiled=True)]
    broadcast_in_dim x2 -> x0, local copies, waits for them, and re-layouts: 1.47 us -> none  [the longest x1 0.8 us: four_steps(): (patch_cell + 7 + 16 * (patch_cell >> 15) & 127)[:, None]]
  transfers between devices with their start and end apart: 8 -> 9, of which waited for: 2 -> 3; matrix products, arithmetic and copies ran while one was open for 2% -> 0% of each run, Pallas kernels for 28% -> 35%
where the time goes in v2:
time: 124 us; the launch traced here: 123 us
  Pallas kernels  57.3 us (46%)
  starting transfers between devices  44.5 us (36%)
  waiting for transfers between devices  17.9 us (14%)
  local copies, waits for them, and re-layouts  2.75 us (2%)
    pallas_call x1, Pallas kernels, four_steps(): pl.pallas_call(steps_kernel, out_shape=(jax.ShapeDtypeStruct((3, 8, 8, NY...  31 us
    ppermute x6, starting transfers between devices, shifted(): return lax.ppermute(array, axis, pairs)  16.2 us
    all_to_all x1, waiting for transfers between devices, slip_response(): lax.all_to_all(sums.reshape(128, 8, 128), ('gx', 'gy'), 0, 0, tiled=True)  10.8 us
    all_to_all x1, starting transfers between devices, per_device(): received = lax.all_to_all(send, ('gx', 'gy'), 0, 0, tiled=True)  10.7 us
    all_to_all x1, starting transfers between devices, slip_response(): lax.all_to_all(sums.reshape(128, 8, 128), ('gx', 'gy'), 0, 0, tiled=True)  10.6 us
    pallas_call x1, Pallas kernels, pack(): pl.pallas_call(pack_kernel, out_shape=(yshape, yshape, qshape), grid=(8,)...  8.35 us
    all_to_all x1, starting transfers between devices, per_device(): gathered = lax.all_to_all(message, 'gy', 0, 0, tiled=True)  6.99 us
    pallas_call x1, Pallas kernels, routed(): small_call(route_kernel, [(tiles, bf16), ((2, 128, 256), bf16), ((2, 128,...  6.33 us
  transfers between devices with their start and end apart: 9, of which 3 were waited for; matrix products, arithmetic and copies ran while one was open for 0% of the time, Pallas kernels for 35%

profile of v2, /device:TPU:1, one launch (start us, length us, event | category | flops | bytes accessed | tf_op | source)
XLA Modules:
  0.0 123.2 jit_solution(2394767575999187473)
XLA Ops:
  0.6 8.4 %pack.1 = (bf16[8,480,128]{2,1,0:T(8,128)(2,1)}, bf16[8,480,128]{2,1,0:T(8,128)(2,1)}, bf16[8,9,32,128]{3,2,1,0:T(8,128)(2,1)}) custom-call(f32[3,8,8,32,128]{4,3,2,1,0:T(8,128)} %bitcast.12, f32[8,8,32,128]{3,2,1,0:T(8,128)} %bitcast.14, f32[8,8,32,128]{3,2,1,0:T(8,128)} %bitcast.16, f32[8,8,32,128]{3,2,1,0:T(8,128)} %bitcast.18, ...), custom_call_target="tpu_custom_call" | custom-call | tf_op jit(solution)/shard_map/pack/pallas_call | solution.py:63
  9.0 4.0 %collective-permute-start = (bf16[8,480,128]{2,1,0:T(8,128)(2,1)}, bf16[8,480,128]{2,1,0:T(8,128)(2,1)S(1)}, u32[]{:S(2)}, u32[]{:S(2)}) collective-permute-start(bf16[8,480,128]{2,1,0:T(8,128)(2,1)} %get-tuple-element.28), channel_id=1, source_target_pairs={{0,1},{1,2},{2,3},{3,4},{4,5},{5,6},{6,7},{7,8},{8,9},{9,10},{10,1... | collective-permute-start | bytes 2949128 | tf_op jit(solution)/shard_map/ppermute | solution.py:77
  13.0 1.3 %collective-permute-start.1 = (bf16[8,480,128]{2,1,0:T(8,128)(2,1)}, bf16[8,480,128]{2,1,0:T(8,128)(2,1)S(1)}, u32[]{:S(2)}, u32[]{:S(2)}) collective-permute-start(bf16[8,480,128]{2,1,0:T(8,128)(2,1)} %get-tuple-element.29), channel_id=1, source_target_pairs={{1,0},{2,1},{3,2},{4,3},{5,4},{6,5},{7,6},{8,7},{9,8},{10,9},{11,1... | collective-permute-start | bytes 2949128 | tf_op jit(solution)/shard_map/ppermute | solution.py:77
  14.3 2.9 %collective-permute-start.3 = (bf16[8,9,32,128]{3,2,1,0:T(8,128)(2,1)}, bf16[8,9,32,128]{3,2,1,0:T(8,128)(2,1)S(1)}, u32[]{:S(2)}, u32[]{:S(2)}) collective-permute-start(bf16[8,9,32,128]{3,2,1,0:T(8,128)(2,1)} %get-tuple-element.30), channel_id=1, source_target_pairs={{16,0},{32,16},{48,32},{64,48},{80,64},{96,80},{112,96},{17,1},{33... | collective-permute-start | bytes 1769480 | tf_op jit(solution)/shard_map/ppermute | solution.py:77
  17.2 3.4 %collective-permute-start.2 = (bf16[8,9,32,128]{3,2,1,0:T(8,128)(2,1)}, bf16[8,9,32,128]{3,2,1,0:T(8,128)(2,1)}, u32[]{:S(2)}, u32[]{:S(2)}) collective-permute-start(bf16[8,9,32,128]{3,2,1,0:T(8,128)(2,1)} %get-tuple-element.30), channel_id=1, source_target_pairs={{0,16},{16,32},{32,48},{48,64},{64,80},{80,96},{96,112},{1,17},{17... | collective-permute-start | bytes 1769480 | tf_op jit(solution)/shard_map/ppermute | solution.py:77
  20.6 6.3 %route.1 = (bf16[128,16,128]{2,1,0:T(8,128)(2,1)}, bf16[2,128,256]{2,1,0:T(8,128)(2,1)}, bf16[2,128,256]{2,1,0:T(8,128)(2,1)}, bf16[256,128]{1,0:T(8,128)(2,1)}, bf16[16,32,256]{2,1,0:T(8,128)(2,1)}) custom-call(s32[64,512]{1,0:T(8,128)} %table.1, f32[256,256]{1,0:T(8,128)} %spectra.2, bf16[256,512]{1,0:T(8,128)(2,1)} %bitcast.27), custom_call_target="tpu_custom_call" | custom-call | tf_op jit(solution)/shard_map/route/pallas_call | solution.py:505
  26.9 10.7 %all-to-all-start = ((bf16[128,16,128]{2,1,0:T(8,128)(2,1)}), bf16[128,16,128]{2,1,0:T(8,128)(2,1)S(1)}, u32[]{:S(2)}, u32[]{:S(2)}) async-start(bf16[128,16,128]{2,1,0:T(8,128)(2,1)} %get-tuple-element.27), calls=%async_computation | async-start | bytes 1048576 | tf_op jit(solution)/shard_map/all_to_all | solution.py:560
  37.7 0.0 collective-permute-done.3.right
  37.7 0.0 copy-start.5
  37.7 0.0 collective-permute-done.2.left
  37.7 0.8 copy-done.5
  38.5 2.3 %join.1 = (bf16[8,9,32,128]{3,2,1,0:T(8,128)(2,1)}, bf16[8,72,128]{2,1,0:T(8,128)(2,1)}, bf16[8,72,128]{2,1,0:T(8,128)(2,1)}) custom-call(bf16[8,9,32,128]{3,2,1,0:T(8,128)(2,1)} %collective-permute-done.2.left, bf16[8,9,32,128]{3,2,1,0:T(8,128)(2,1)} %copy-done.5), custom_call_target="tpu_custom_call" | custom-call | tf_op jit(solution)/shard_map/join/pallas_call | solution.py:358
  40.8 3.3 %collective-permute-start.4 = (bf16[8,72,128]{2,1,0:T(8,128)(2,1)}, bf16[8,72,128]{2,1,0:T(8,128)(2,1)S(1)}, u32[]{:S(2)}, u32[]{:S(2)}) collective-permute-start(bf16[8,72,128]{2,1,0:T(8,128)(2,1)} %get-tuple-element.32), channel_id=1, source_target_pairs={{0,1},{1,2},{2,3},{3,4},{4,5},{5,6},{6,7},{7,8},{8,9},{9,10},{10,1... | collective-permute-start | bytes 442376 | tf_op jit(solution)/shard_map/ppermute | solution.py:77
  44.1 1.3 %collective-permute-start.5 = (bf16[8,72,128]{2,1,0:T(8,128)(2,1)}, bf16[8,72,128]{2,1,0:T(8,128)(2,1)S(1)}, u32[]{:S(2)}, u32[]{:S(2)}) collective-permute-start(bf16[8,72,128]{2,1,0:T(8,128)(2,1)} %get-tuple-element.33), channel_id=1, source_target_pairs={{1,0},{2,1},{3,2},{4,3},{5,4},{6,5},{7,6},{8,7},{9,8},{10,9},{11,1... | collective-permute-start | bytes 442376 | tf_op jit(solution)/shard_map/ppermute | solution.py:77
  45.4 6.2 %all-to-all-done.received = bf16[128,16,128]{2,1,0:T(8,128)(2,1)S(1)} async-done(((bf16[128,16,128]{2,1,0:T(8,128)(2,1)}), bf16[128,16,128]{2,1,0:T(8,128)(2,1)S(1)}, u32[]{:S(2)}, u32[]{:S(2)}) %all-to-all-start) | async-done | bytes 524320 | tf_op jit(solution)/shard_map/all_to_all | solution.py:560
  51.6 0.0 collective-permute-done.4.cprev
  51.6 0.0 collective-permute-done.5.cnext
  51.6 0.0 copy-start.7
  51.6 0.0 collective-permute-done.yprev
  51.6 0.0 copy-start.3
  51.7 0.0 collective-permute-done.1.ynext
  51.7 1.1 copy-done.1
  52.8 3.9 %sort.1 = (bf16[16,288,256]{2,1,0:T(8,128)(2,1)}, bf16[256,512]{1,0:T(8,128)(2,1)}) custom-call(bf16[128,16,128]{2,1,0:T(8,128)(2,1)} %copy-done.1, bf16[2,128,256]{2,1,0:T(8,128)(2,1)} %get-tuple-element.35.place, bf16[2,128,256]{2,1,0:T(8,128)(2,1)} %get-tuple-element.36.pick, bf16[16,32,256]{2,1,0:T(8,128)(2,1)} %get-tuple-element.37.turned), custom_call_target="tpu_custom_call" | custom-call | tf_op jit(solution)/shard_map/sort/pallas_call | solution.py:522
  56.7 0.0 copy-done.4
  56.7 7.0 %all-to-all-start.1 = ((bf16[16,288,256]{2,1,0:T(8,128)(2,1)}), bf16[16,288,256]{2,1,0:T(8,128)(2,1)S(1)}, u32[]{:S(2)}, u32[]{:S(2)}) async-start(bf16[16,288,256]{2,1,0:T(8,128)(2,1)} %get-tuple-element.38), calls=%async_computation.1 | async-start | bytes 4718592 | tf_op jit(solution)/shard_map/all_to_all | solution.py:563
  63.7 31.0 %four_steps.1 = (f32[3,8,8,32,128]{4,3,2,1,0:T(8,128)}, f32[8,8,32,128]{3,2,1,0:T(8,128)}, f32[8,8,32,128]{3,2,1,0:T(8,128)}, f32[256,256]{1,0:T(8,128)}, f32[8,16,8,128]{3,2,1,0:T(8,128)}) custom-call(s32[256]{0:T(256)} %cell.1, f32[3,8,8,32,128]{4,3,2,1,0:T(8,128)} %bitcast.13, f32[8,8,32,128]{3,2,1,0:T(8,128)} %bitcast.15, f32[8,8,32,128]{3,2,1,0:T(8,128)} %bitcast.17, ...), custom_call_target="tpu_custom_call" | custom-call | tf_op jit(solution)/shard_map/four_steps/pallas_call | solution.py:300
  94.7 0.8 all-to-all-done.1.gathered
  95.6 10.6 %all-to-all-start.2 = ((f32[128,8,128]{2,1,0:T(8,128)}), f32[128,8,128]{2,1,0:T(8,128)S(1)}, u32[]{:S(2)}, u32[]{:S(2)}) async-start(f32[128,8,128]{2,1,0:T(8,128)} %bitcast.26), calls=%async_computation.2 | async-start | bytes 1048576 | tf_op jit(solution)/shard_map/all_to_all | solution.py:535
  106.2 3.1 %product.1 = f32[256,256]{1,0:T(8,128)} custom-call(bf16[16,288,256]{2,1,0:T(8,128)(2,1)} %copy-done), custom_call_target="tpu_custom_call" | custom-call | tf_op jit(solution)/shard_map/product/pallas_call | solution.py:536
  109.3 10.8 %all-to-all-done.2.sums = f32[128,8,128]{2,1,0:T(8,128)S(1)} async-done(((f32[128,8,128]{2,1,0:T(8,128)}), f32[128,8,128]{2,1,0:T(8,128)S(1)}, u32[]{:S(2)}, u32[]{:S(2)}) %all-to-all-start.2) | async-done | bytes 524320 | tf_op jit(solution)/shard_map/all_to_all | solution.py:535
  120.1 0.8 copy-done.2
  120.9 2.3 %slip.1 = f32[8,32,256]{2,1,0:T(8,128)} custom-call(f32[256,256]{1,0:T(8,128)} %product.1, f32[128,8,128]{2,1,0:T(8,128)} %copy-done.2, f32[128,256]{1,0:T(8,128)} %constant.5.clone.phase), custom_call_target="tpu_custom_call" | custom-call | tf_op jit(solution)/shard_map/slip/pallas_call | solution.py:538
  (9 shorter events, 0.0 us)
Async XLA Ops:
  9.0 42.7 %collective-permute-start = (bf16[8,480,128]{2,1,0:T(8,128)(2,1)}, bf16[8,480,128]{2,1,0:T(8,128)(2,1)S(1)}, u32[]{:S(2)}, u32[]{:S(2)}) collective-permute-start(bf16[8,480,128]{2,1,0:T(8,128)(2,1)} %get-tuple-element.28), channel_id=1, source_target_pairs={{0,1},{1,2},{2,3},{3,4},{4,5},{5,6},{6,7},{7,8},{8,9},{9,10},{10,1... | collective-permute-start | bytes 2949128 | tf_op jit(solution)/shard_map/ppermute | solution.py:77
  13.0 38.7 %collective-permute-start.1 = (bf16[8,480,128]{2,1,0:T(8,128)(2,1)}, bf16[8,480,128]{2,1,0:T(8,128)(2,1)S(1)}, u32[]{:S(2)}, u32[]{:S(2)}) collective-permute-start(bf16[8,480,128]{2,1,0:T(8,128)(2,1)} %get-tuple-element.29), channel_id=1, source_target_pairs={{1,0},{2,1},{3,2},{4,3},{5,4},{6,5},{7,6},{8,7},{9,8},{10,9},{11,1... | collective-permute-start | bytes 2949128 | tf_op jit(solution)/shard_map/ppermute | solution.py:77
  14.3 23.4 %collective-permute-start.3 = (bf16[8,9,32,128]{3,2,1,0:T(8,128)(2,1)}, bf16[8,9,32,128]{3,2,1,0:T(8,128)(2,1)S(1)}, u32[]{:S(2)}, u32[]{:S(2)}) collective-permute-start(bf16[8,9,32,128]{3,2,1,0:T(8,128)(2,1)} %get-tuple-element.30), channel_id=1, source_target_pairs={{16,0},{32,16},{48,32},{64,48},{80,64},{96,80},{112,96},{17,1},{33... | collective-permute-start | bytes 1769480 | tf_op jit(solution)/shard_map/ppermute | solution.py:77
  17.2 20.6 %collective-permute-start.2 = (bf16[8,9,32,128]{3,2,1,0:T(8,128)(2,1)}, bf16[8,9,32,128]{3,2,1,0:T(8,128)(2,1)}, u32[]{:S(2)}, u32[]{:S(2)}) collective-permute-start(bf16[8,9,32,128]{3,2,1,0:T(8,128)(2,1)} %get-tuple-element.30), channel_id=1, source_target_pairs={{0,16},{16,32},{32,48},{48,64},{64,80},{80,96},{96,112},{1,17},{17... | collective-permute-start | bytes 1769480 | tf_op jit(solution)/shard_map/ppermute | solution.py:77
  26.9 24.7 %all-to-all-start = ((bf16[128,16,128]{2,1,0:T(8,128)(2,1)}), bf16[128,16,128]{2,1,0:T(8,128)(2,1)S(1)}, u32[]{:S(2)}, u32[]{:S(2)}) async-start(bf16[128,16,128]{2,1,0:T(8,128)(2,1)} %get-tuple-element.27), calls=%async_computation | async-start | bytes 1048576 | tf_op jit(solution)/shard_map/all_to_all | solution.py:560
  37.7 0.8 copy-start.5
  40.8 10.8 %collective-permute-start.4 = (bf16[8,72,128]{2,1,0:T(8,128)(2,1)}, bf16[8,72,128]{2,1,0:T(8,128)(2,1)S(1)}, u32[]{:S(2)}, u32[]{:S(2)}) collective-permute-start(bf16[8,72,128]{2,1,0:T(8,128)(2,1)} %get-tuple-element.32), channel_id=1, source_target_pairs={{0,1},{1,2},{2,3},{3,4},{4,5},{5,6},{6,7},{7,8},{8,9},{9,10},{10,1... | collective-permute-start | bytes 442376 | tf_op jit(solution)/shard_map/ppermute | solution.py:77
  44.1 7.5 %collective-permute-start.5 = (bf16[8,72,128]{2,1,0:T(8,128)(2,1)}, bf16[8,72,128]{2,1,0:T(8,128)(2,1)S(1)}, u32[]{:S(2)}, u32[]{:S(2)}) collective-permute-start(bf16[8,72,128]{2,1,0:T(8,128)(2,1)} %get-tuple-element.33), channel_id=1, source_target_pairs={{1,0},{2,1},{3,2},{4,3},{5,4},{6,5},{7,6},{8,7},{9,8},{10,9},{11,1... | collective-permute-start | bytes 442376 | tf_op jit(solution)/shard_map/ppermute | solution.py:77
  51.6 1.2 copy-start.1
  51.6 12.0 %copy-start.6 = (bf16[8,72,128]{2,1,0:T(8,128)(2,1)}, bf16[8,72,128]{2,1,0:T(8,128)(2,1)S(1)}, u32[]{:S(2)}) copy-start(bf16[8,72,128]{2,1,0:T(8,128)(2,1)S(1)} %collective-permute-done.4.cprev) | copy-start | bytes 442372
  51.6 5.0 %copy-start.7 = (bf16[8,72,128]{2,1,0:T(8,128)(2,1)}, bf16[8,72,128]{2,1,0:T(8,128)(2,1)S(1)}, u32[]{:S(2)}) copy-start(bf16[8,72,128]{2,1,0:T(8,128)(2,1)S(1)} %collective-permute-done.5.cnext) | copy-start | bytes 442372
  51.6 12.0 %copy-start.3 = (bf16[8,480,128]{2,1,0:T(8,128)(2,1)}, bf16[8,480,128]{2,1,0:T(8,128)(2,1)S(1)}, u32[]{:S(2)}) copy-start(bf16[8,480,128]{2,1,0:T(8,128)(2,1)S(1)} %collective-permute-done.yprev) | copy-start | bytes 2949124
  51.7 5.0 %copy-start.4 = (bf16[8,480,128]{2,1,0:T(8,128)(2,1)}, bf16[8,480,128]{2,1,0:T(8,128)(2,1)S(1)}, u32[]{:S(2)}) copy-start(bf16[8,480,128]{2,1,0:T(8,128)(2,1)S(1)} %collective-permute-done.1.ynext) | copy-start | bytes 2949124
  56.7 38.9 %all-to-all-start.1 = ((bf16[16,288,256]{2,1,0:T(8,128)(2,1)}), bf16[16,288,256]{2,1,0:T(8,128)(2,1)S(1)}, u32[]{:S(2)}, u32[]{:S(2)}) async-start(bf16[16,288,256]{2,1,0:T(8,128)(2,1)} %get-tuple-element.38), calls=%async_computation.1 | async-start | bytes 4718592 | tf_op jit(solution)/shard_map/all_to_all | solution.py:563
  95.6 10.6 %copy-start = (bf16[16,288,256]{2,1,0:T(8,128)(2,1)}, bf16[16,288,256]{2,1,0:T(8,128)(2,1)S(1)}, u32[]{:S(2)}) copy-start(bf16[16,288,256]{2,1,0:T(8,128)(2,1)S(1)} %all-to-all-done.1.gathered) | copy-start | bytes 7077892
  95.6 24.5 %all-to-all-start.2 = ((f32[128,8,128]{2,1,0:T(8,128)}), f32[128,8,128]{2,1,0:T(8,128)S(1)}, u32[]{:S(2)}, u32[]{:S(2)}) async-start(f32[128,8,128]{2,1,0:T(8,128)} %bitcast.26), calls=%async_computation.2 | async-start | bytes 1048576 | tf_op jit(solution)/shard_map/all_to_all | solution.py:535
  120.1 0.8 copy-start.2

commit v3 on v2

--- a/solution.py
+++ b/solution.py
@@ -14,6 +14,7 @@
 FIELDS = 9
 VX, VY, VZ, PR, ME, BU, MO, RE, ST = range(FIELDS)
 BP = FIELDS
+AHEAD = 6
 REACH = [7, 7, 6, 8, 6, 7, 6, 6, 6]
 SENT = [(f, d) for f in range(FIELDS) for d in range(REACH[f])]
 ROWS = 8 * (len(SENT) + len(SENT) % 2)
@@ -28,47 +29,97 @@
     return pltpu.roll(x, shift, axis) if shift else x
 
 
-def pack_kernel(vel, pr, me, bu, mo, re, st, lo_ref, hi_ref, q_ref, lows, highs):
+def pack_kernel(
+    vel, pr, me, bu, mo, re, st, turn, lo_o, hi_o, q_o, X, lo_s, hi_s, q_s, lows, highs, sems, done
+):
+    sources = [vel.at[0], vel.at[1], vel.at[2], pr, me, bu, mo, re, st]
+
+    def fetch(zi):
+        return [
+            pltpu.make_async_copy(src.at[:, zi], X.at[f, :, zi], sems.at[f, zi])
+            for f, src in enumerate(sources)
+        ]
+
+    def put(zi):
+        return [
+            pltpu.make_async_copy(src.at[zi], dst.at[zi], done.at[k, zi])
+            for k, (src, dst) in enumerate(((lo_s, lo_o), (hi_s, hi_o), (q_s, q_o)))
+        ]
+
+    for zi in range(AHEAD):
+        for c in fetch(zi):
+            c.start()
     lane = lanes((NY, 128))
-    fields = [vel.at[0], vel.at[1], vel.at[2], pr, me, bu, mo, re, st]
-    for f, ref in enumerate(fields):
-        strip = jnp.zeros((NY, 128), jnp.float32)
+
+    def one(zi, _):
+        @pl.when(zi + AHEAD < 8)
+        def _():
+            for c in fetch(zi + AHEAD):
+                c.start()
+
+        copies = fetch(zi)
+        for c in copies:
+            c.wait()
+        strips = jnp.zeros((FIELDS * NY, 128), jnp.float32)
         for g in range(8):
-            turned = roll(ref[g, 0], 8 + 16 * g)
-            strip = jnp.where((lane >> 4) == g, turned, strip)
-            low, high = turned[:HALO], turned[NY - HALO :]
-            if f == VX:
-                low, high = roll(low, -1), roll(high, -1)
-            lows[f, pl.ds(8 * g, 8)] = low
-            highs[f, pl.ds(8 * g, 8)] = high
-        q_ref[0, f] = strip.astype(jnp.bfloat16)
-    for ref, ends, first in ((lo_ref, lows, False), (hi_ref, highs, True)):
-        tiles = [
-            ends[f, pl.ds(d + (HALO - REACH[f] if first else 0), 8, stride=8)] for f, d in SENT
-        ]
-        if len(tiles) % 2:
-            tiles.append(tiles[-1])
-        for t in range(0, len(tiles), 2):
-            pair = jnp.concatenate(tiles[t : t + 2], axis=0)
-            ref[0, pl.ds(8 * t, 16)] = pair.astype(jnp.bfloat16)
+            planes = [X[f, g, zi] for f in range(FIELDS)]
+            for f, plane in enumerate(planes):
+                shift = (7 if f == VX else 8) + 16 * g
+                lows[f, pl.ds(8 * g, 8)] = roll(plane[:HALO], shift)
+                highs[f, pl.ds(8 * g, 8)] = roll(plane[NY - HALO :], shift)
+            planes = jnp.concatenate(planes, axis=0).astype(jnp.bfloat16)
+            strips += jnp.dot(planes, turn[g], preferred_element_type=jnp.float32)
+        q_s[zi] = strips.astype(jnp.bfloat16).reshape(FIELDS, NY, 128)
+        for ref, ends, first in ((lo_s, lows, False), (hi_s, highs, True)):
+            tiles = [
+                ends[f, pl.ds(d + (HALO - REACH[f] if first else 0), 8, stride=8)]
+                for f, d in SENT
+            ]
+            if len(tiles) % 2:
+                tiles.append(tiles[-1])
+            for t in range(0, len(tiles), 2):
+                pair = jnp.concatenate(tiles[t : t + 2], axis=0)
+                ref[zi, pl.ds(8 * t, 16)] = pair.astype(jnp.bfloat16)
+        for c in put(zi):
+            c.start()
+        return 0
+
+    lax.fori_loop(0, 8, one, 0)
+    for zi in range(8):
+        for c in put(zi):
+            c.wait()
 
 
 def pack(velocity, *fields):
-    spec = pl.BlockSpec((8, 1, NY, NX), lambda i: (0, i, 0, 0))
-    vspec = pl.BlockSpec((3, 8, 1, NY, NX), lambda i: (0, 0, i, 0, 0))
-    yspec = pl.BlockSpec((1, ROWS, 128), lambda i: (i, 0, 0))
-    qspec = pl.BlockSpec((1, FIELDS, NY, 128), lambda i: (i, 0, 0, 0))
-    yshape = jax.ShapeDtypeStruct((8, ROWS, 128), jnp.bfloat16)
-    qshape = jax.ShapeDtypeStruct((8, FIELDS, NY, 128), jnp.bfloat16)
+    lane = np.arange(128)
+    turn = np.zeros((8, 128, 128), np.float32)
+    for g in range(8):
+        own = lane[lane >> 4 == g]
+        turn[g, (own - 8 - 16 * g) % 128, own] = 1
+    any_spec = pl.BlockSpec(memory_space=pl.ANY)
+    yshape, qshape = (8, ROWS, 128), (8, FIELDS, NY, 128)
     return pl.pallas_call(
         pack_kernel,
-        out_shape=(yshape, yshape, qshape),
-        grid=(8,),
-        in_specs=[vspec] + [spec] * 6,
-        out_specs=(yspec, yspec, qspec),
-        scratch_shapes=[pltpu.VMEM((FIELDS, 64, 128), jnp.float32)] * 2,
+        out_shape=tuple(jax.ShapeDtypeStruct(s, jnp.bfloat16) for s in (yshape, yshape, qshape)),
+        in_specs=[any_spec] * 7 + [pl.BlockSpec(memory_space=pltpu.VMEM)],
+        out_specs=(any_spec,) * 3,
+        scratch_shapes=[
+            pltpu.VMEM((FIELDS, 8, 8, NY, 128), jnp.float32),
+            pltpu.VMEM(yshape, jnp.bfloat16),
+            pltpu.VMEM(yshape, jnp.bfloat16),
+            pltpu.VMEM(qshape, jnp.bfloat16),
+            pltpu.VMEM((FIELDS, 64, 128), jnp.float32),
+            pltpu.VMEM((FIELDS, 64, 128), jnp.float32),
+            pltpu.SemaphoreType.DMA((FIELDS, 8)),
+            pltpu.SemaphoreType.DMA((3, 8)),
+        ],
+        compiler_params=pltpu.CompilerParams(vmem_limit_bytes=56 * 1024 * 1024),
         name="pack",
-    )(velocity.reshape(3, 8, 8, NY, NX), *[f.reshape(8, 8, NY, NX) for f in fields])
+    )(
+        velocity.reshape(3, 8, 8, NY, NX),
+        *[f.reshape(8, 8, NY, NX) for f in fields],
+        jnp.asarray(turn, jnp.bfloat16),
+    )
 
 
 def shifted(array, axis, up):
@@ -122,12 +173,15 @@
     sems,
 ):
     sources = [vel.at[0], vel.at[1], vel.at[2], pr, me, bu, mo, re, st]
-    copies = [
-        [pltpu.make_async_copy(src.at[:, zi], X.at[f, :, zi], sems.at[f, zi]) for f, src in enumerate(sources)]
-        for zi in range(8)
-    ]
-    for row in copies:
-        for c in row:
+
+    def fetch(zi):
+        return [
+            pltpu.make_async_copy(src.at[:, zi], X.at[f, :, zi], sems.at[f, zi])
+            for f, src in enumerate(sources)
+        ]
+
+    for zi in range(AHEAD):
+        for c in fetch(zi):
             c.start()
     lane = lanes((EY, 128))
     lane16 = lane & 15
@@ -175,10 +229,18 @@
             E[f, 10 * g + 9] = roll(E[f, 10 * g + 11], -16) if g < 7 else zero
 
     T[...] = jnp.zeros_like(T)
-    for zi in range(8):
-        for c in copies[zi]:
+    def load(zi, _):
+        @pl.when(zi + AHEAD < 8)
+        def _():
+            for c in fetch(zi + AHEAD):
+                c.start()
+
+        for c in fetch(zi):
             c.wait()
         fill(zi)
+        return 0
+
+    lax.fori_loop(0, 8, load, 0)
     wrap_planes(PR)
 
     def moved(ref, z, dx, p):
@@ -244,14 +306,23 @@
     lax.fori_loop(0, STEPS - 1, lambda n, _: step(n, False), 0)
     step(STEPS - 1, True)
     targets = [vel_o.at[0], vel_o.at[1], vel_o.at[2], pr_o, me_o]
-    outs = []
-    for zi in range(8):
-        for f, dst in enumerate(targets):
+
+    def put(zi):
+        return [
+            pltpu.make_async_copy(X.at[f, :, zi], dst.at[:, zi], sems.at[f, zi])
+            for f, dst in enumerate(targets)
+        ]
+
+    def unload(zi, _):
+        for f in range(len(targets)):
             for g in range(8):
                 plane = E[f, g * 10 + zi + 1, HALO : HALO + NY]
                 X[f, g, zi] = roll(plane, -(7 if f == VX else 8) - 16 * g)
-            outs.append(pltpu.make_async_copy(X.at[f, :, zi], dst.at[:, zi], sems.at[f, zi]))
-            outs[-1].start()
+        for c in put(zi):
+            c.start()
+        return 0
+
+    lax.fori_loop(0, 8, unload, 0)
 
     def pick(i, _):
         for k in range(8):
@@ -283,8 +354,9 @@
         for n in range(STEPS):
             packed = jnp.where(quarter == n, roll(sums[n][:, block], 32 * (n - j % 4)), packed)
         sums_o[:, j] = packed.reshape(8, 8, 128)
-    for c in outs:
-        c.wait()
+    for zi in range(8):
+        for c in put(zi):
+            c.wait()
 
 
 def phase_rows(freqs):
@@ -336,7 +408,8 @@
 
 def join_kernel(left, right, side, low, high):
     from_left = (lanes((NY, 128)) & 15) < 8
-    for zi in range(8):
+
+    def one(zi, _):
         lows, highs = [], []
         for f in range(FIELDS):
             strip = jnp.where(
@@ -347,6 +420,9 @@
             highs.append(strip[NY - HALO :])
         low[zi] = jnp.concatenate(lows, axis=0).astype(jnp.bfloat16)
         high[zi] = jnp.concatenate(highs, axis=0).astype(jnp.bfloat16)
+        return 0
+
+    lax.fori_loop(0, 8, one, 0)
 
 
 def halo_exchange(velocity, fields):
@@ -440,20 +516,22 @@
         sent = jnp.dot(to, rounded, preferred_element_type=jnp.float32)
         sent_w = jnp.dot(back, weights[...], preferred_element_type=jnp.float32)
         for c in range(2):
-            stage[:, 6 * k + c, :] = sent[:, 128 * c : 128 * (c + 1)]
+            stage[pl.ds(6 * k + c, 128, stride=16), :] = sent[:, 128 * c : 128 * (c + 1)]
         for c in range(4):
-            stage[:, 6 * k + 2 + c, :] = sent_w[:, 128 * c : 128 * (c + 1)]
-    send[...] = stage[...].astype(jnp.bfloat16)
+            stage[pl.ds(6 * k + 2 + c, 128, stride=16), :] = sent_w[:, 128 * c : 128 * (c + 1)]
+    send[...] = stage[...].astype(jnp.bfloat16).reshape(send.shape)
     eye = (rows_of((n, n)) == lanes((n, n))).astype(jnp.float32).astype(jnp.bfloat16)
     turned[...] = transposed_dot(weights[...], eye).astype(jnp.bfloat16).reshape(turned.shape)
 
 
 def sort_kernel(received, place, pick, turned, message, patch_weights, stage):
-    stage[...] = received[...].astype(jnp.float32)
+    stage[...] = received[...].reshape(stage.shape).astype(jnp.float32)
     spectra = jnp.zeros((256, 256), jnp.float32)
     mine = jnp.zeros((256, 512), jnp.float32)
     for k in range(CAP):
-        parts = [stage[:, 6 * k + c, :].astype(jnp.bfloat16) for c in range(6)]
+        parts = [
+            stage[pl.ds(6 * k + c, 128, stride=16), :].astype(jnp.bfloat16) for c in range(6)
+        ]
         spectra += transposed_dot(pick[k], jnp.concatenate(parts[:2], axis=1))
         mine += transposed_dot(place[k], jnp.concatenate(parts[2:], axis=1))
     patch_weights[...] = mine.astype(jnp.bfloat16)
@@ -512,7 +590,7 @@
             ((16, 32, 256), bf16),
         ],
         "route",
-        [pltpu.VMEM(tiles, f32)],
+        [pltpu.VMEM((2048, 128), f32)],
         0,
         3,
     )(rupture_patches, spectra, slip_weights.reshape(256, 512))
@@ -523,7 +601,7 @@
         sort_kernel,
         [((16, 288, 256), jnp.bfloat16), ((256, 512), jnp.bfloat16)],
         "sort",
-        [pltpu.VMEM(received.shape, jnp.float32)],
+        [pltpu.VMEM((2048, 128), jnp.float32)],
         0,
         4,
     )(received, place, pick, turned)

time: 124 us -> 123 us (level)
  Pallas kernels: 57.3 us -> 56 us
where the time goes in v3:
time: 123 us; the launch traced here: 122 us
  Pallas kernels  56 us (46%)
  starting transfers between devices  45.1 us (37%)
  waiting for transfers between devices  17.3 us (14%)
  local copies, waits for them, and re-layouts  2.75 us (2%)
    pallas_call x1, Pallas kernels, four_steps(): pl.pallas_call(steps_kernel, out_shape=(jax.ShapeDtypeStruct((3, 8, 8, NY...  31.6 us
    ppermute x6, starting transfers between devices, shifted(): return lax.ppermute(array, axis, pairs)  16.2 us
    all_to_all x1, starting transfers between devices, slip_response(): lax.all_to_all(sums.reshape(128, 8, 128), ('gx', 'gy'), 0, 0, tiled=True)  11.1 us
    all_to_all x1, waiting for transfers between devices, slip_response(): lax.all_to_all(sums.reshape(128, 8, 128), ('gx', 'gy'), 0, 0, tiled=True)  10.8 us
    all_to_all x1, starting transfers between devices, per_device(): received = lax.all_to_all(send, ('gx', 'gy'), 0, 0, tiled=True)  10.7 us
    pallas_call x1, Pallas kernels, pack(): pl.pallas_call(pack_kernel, out_shape=tuple((jax.ShapeDtypeStruct(s, jnp....  7.3 us
    all_to_all x1, starting transfers between devices, per_device(): gathered = lax.all_to_all(message, 'gy', 0, 0, tiled=True)  7.06 us
    all_to_all x1, waiting for transfers between devices, per_device(): received = lax.all_to_all(send, ('gx', 'gy'), 0, 0, tiled=True)  6.15 us
  transfers between devices with their start and end apart: 9, of which 3 were waited for; matrix products, arithmetic and copies ran while one was open for 0% of the time, Pallas kernels for 35%

profile of v3, /device:TPU:1, one launch (start us, length us, event | category | flops | bytes accessed | tf_op | source)
XLA Modules:
  0.0 122.0 jit_solution(14470684531110313693)
XLA Ops:
  0.6 7.3 %pack.1 = (bf16[8,480,128]{2,1,0:T(8,128)(2,1)}, bf16[8,480,128]{2,1,0:T(8,128)(2,1)}, bf16[8,9,32,128]{3,2,1,0:T(8,128)(2,1)}) custom-call(f32[3,8,8,32,128]{4,3,2,1,0:T(8,128)} %bitcast.12, f32[8,8,32,128]{3,2,1,0:T(8,128)} %bitcast.14, f32[8,8,32,128]{3,2,1,0:T(8,128)} %bitcast.16, f32[8,8,32,128]{3,2,1,0:T(8,128)} %bitcast.18, ...), custom_call_target="tpu_custom_call" | custom-call | tf_op jit(solution)/shard_map/pack/pallas_call | solution.py:101
  7.9 4.0 %collective-permute-start = (bf16[8,480,128]{2,1,0:T(8,128)(2,1)}, bf16[8,480,128]{2,1,0:T(8,128)(2,1)S(1)}, u32[]{:S(2)}, u32[]{:S(2)}) collective-permute-start(bf16[8,480,128]{2,1,0:T(8,128)(2,1)} %get-tuple-element.28), channel_id=1, source_target_pairs={{0,1},{1,2},{2,3},{3,4},{4,5},{5,6},{6,7},{7,8},{8,9},{9,10},{10,1... | collective-permute-start | bytes 2949128 | tf_op jit(solution)/shard_map/ppermute | solution.py:128
  12.0 1.3 %collective-permute-start.1 = (bf16[8,480,128]{2,1,0:T(8,128)(2,1)}, bf16[8,480,128]{2,1,0:T(8,128)(2,1)S(1)}, u32[]{:S(2)}, u32[]{:S(2)}) collective-permute-start(bf16[8,480,128]{2,1,0:T(8,128)(2,1)} %get-tuple-element.29), channel_id=1, source_target_pairs={{1,0},{2,1},{3,2},{4,3},{5,4},{6,5},{7,6},{8,7},{9,8},{10,9},{11,1... | collective-permute-start | bytes 2949128 | tf_op jit(solution)/shard_map/ppermute | solution.py:128
  13.3 2.9 %collective-permute-start.3 = (bf16[8,9,32,128]{3,2,1,0:T(8,128)(2,1)}, bf16[8,9,32,128]{3,2,1,0:T(8,128)(2,1)S(1)}, u32[]{:S(2)}, u32[]{:S(2)}) collective-permute-start(bf16[8,9,32,128]{3,2,1,0:T(8,128)(2,1)} %get-tuple-element.30), channel_id=1, source_target_pairs={{16,0},{32,16},{48,32},{64,48},{80,64},{96,80},{112,96},{17,1},{33... | collective-permute-start | bytes 1769480 | tf_op jit(solution)/shard_map/ppermute | solution.py:128
  16.1 3.4 %collective-permute-start.2 = (bf16[8,9,32,128]{3,2,1,0:T(8,128)(2,1)}, bf16[8,9,32,128]{3,2,1,0:T(8,128)(2,1)}, u32[]{:S(2)}, u32[]{:S(2)}) collective-permute-start(bf16[8,9,32,128]{3,2,1,0:T(8,128)(2,1)} %get-tuple-element.30), channel_id=1, source_target_pairs={{0,16},{16,32},{32,48},{48,64},{64,80},{80,96},{96,112},{1,17},{17... | collective-permute-start | bytes 1769480 | tf_op jit(solution)/shard_map/ppermute | solution.py:128
  19.6 6.1 %route.1 = (bf16[128,16,128]{2,1,0:T(8,128)(2,1)}, bf16[2,128,256]{2,1,0:T(8,128)(2,1)}, bf16[2,128,256]{2,1,0:T(8,128)(2,1)}, bf16[256,128]{1,0:T(8,128)(2,1)}, bf16[16,32,256]{2,1,0:T(8,128)(2,1)}) custom-call(s32[64,512]{1,0:T(8,128)} %table.1, f32[256,256]{1,0:T(8,128)} %spectra.2, bf16[256,512]{1,0:T(8,128)(2,1)} %bitcast.27), custom_call_target="tpu_custom_call" | custom-call | tf_op jit(solution)/shard_map/route/pallas_call | solution.py:583
  25.7 10.7 %all-to-all-start = ((bf16[128,16,128]{2,1,0:T(8,128)(2,1)}), bf16[128,16,128]{2,1,0:T(8,128)(2,1)S(1)}, u32[]{:S(2)}, u32[]{:S(2)}) async-start(bf16[128,16,128]{2,1,0:T(8,128)(2,1)} %get-tuple-element.27), calls=%async_computation | async-start | bytes 1048576 | tf_op jit(solution)/shard_map/all_to_all | solution.py:638
  36.4 0.0 collective-permute-done.3.right
  36.4 0.0 copy-start.5
  36.4 0.0 collective-permute-done.2.left
  36.4 0.8 copy-done.5
  37.3 2.3 %join.1 = (bf16[8,9,32,128]{3,2,1,0:T(8,128)(2,1)}, bf16[8,72,128]{2,1,0:T(8,128)(2,1)}, bf16[8,72,128]{2,1,0:T(8,128)(2,1)}) custom-call(bf16[8,9,32,128]{3,2,1,0:T(8,128)(2,1)} %collective-permute-done.2.left, bf16[8,9,32,128]{3,2,1,0:T(8,128)(2,1)} %copy-done.5), custom_call_target="tpu_custom_call" | custom-call | tf_op jit(solution)/shard_map/join/pallas_call | solution.py:434
  39.6 3.3 %collective-permute-start.4 = (bf16[8,72,128]{2,1,0:T(8,128)(2,1)}, bf16[8,72,128]{2,1,0:T(8,128)(2,1)S(1)}, u32[]{:S(2)}, u32[]{:S(2)}) collective-permute-start(bf16[8,72,128]{2,1,0:T(8,128)(2,1)} %get-tuple-element.32), channel_id=1, source_target_pairs={{0,1},{1,2},{2,3},{3,4},{4,5},{5,6},{6,7},{7,8},{8,9},{9,10},{10,1... | collective-permute-start | bytes 442376 | tf_op jit(solution)/shard_map/ppermute | solution.py:128
  42.9 1.3 %collective-permute-start.5 = (bf16[8,72,128]{2,1,0:T(8,128)(2,1)}, bf16[8,72,128]{2,1,0:T(8,128)(2,1)S(1)}, u32[]{:S(2)}, u32[]{:S(2)}) collective-permute-start(bf16[8,72,128]{2,1,0:T(8,128)(2,1)} %get-tuple-element.33), channel_id=1, source_target_pairs={{1,0},{2,1},{3,2},{4,3},{5,4},{6,5},{7,6},{8,7},{9,8},{10,9},{11,1... | collective-permute-start | bytes 442376 | tf_op jit(solution)/shard_map/ppermute | solution.py:128
  44.2 6.2 %all-to-all-done.received = bf16[128,16,128]{2,1,0:T(8,128)(2,1)S(1)} async-done(((bf16[128,16,128]{2,1,0:T(8,128)(2,1)}), bf16[128,16,128]{2,1,0:T(8,128)(2,1)S(1)}, u32[]{:S(2)}, u32[]{:S(2)}) %all-to-all-start) | async-done | bytes 524320 | tf_op jit(solution)/shard_map/all_to_all | solution.py:638
  50.3 0.0 collective-permute-done.4.cprev
  50.3 0.0 collective-permute-done.5.cnext
  50.4 0.0 collective-permute-done.yprev
  50.4 0.0 collective-permute-done.1.ynext
  50.4 0.0 copy-start.4
  50.4 1.1 copy-done.1
  51.5 3.3 %sort.1 = (bf16[16,288,256]{2,1,0:T(8,128)(2,1)}, bf16[256,512]{1,0:T(8,128)(2,1)}) custom-call(bf16[128,16,128]{2,1,0:T(8,128)(2,1)} %copy-done.1, bf16[2,128,256]{2,1,0:T(8,128)(2,1)} %get-tuple-element.35.place, bf16[2,128,256]{2,1,0:T(8,128)(2,1)} %get-tuple-element.36.pick, bf16[16,32,256]{2,1,0:T(8,128)(2,1)} %get-tuple-element.37.turned), custom_call_target="tpu_custom_call" | custom-call | tf_op jit(solution)/shard_map/sort/pallas_call | solution.py:600
  54.8 7.1 %all-to-all-start.1 = ((bf16[16,288,256]{2,1,0:T(8,128)(2,1)}), bf16[16,288,256]{2,1,0:T(8,128)(2,1)S(1)}, u32[]{:S(2)}, u32[]{:S(2)}) async-start(bf16[16,288,256]{2,1,0:T(8,128)(2,1)} %get-tuple-element.38), calls=%async_computation.1 | async-start | bytes 4718592 | tf_op jit(solution)/shard_map/all_to_all | solution.py:641
  61.9 0.0 copy-done.6
  61.9 0.0 copy-done.3
  61.9 31.6 %four_steps.1 = (f32[3,8,8,32,128]{4,3,2,1,0:T(8,128)}, f32[8,8,32,128]{3,2,1,0:T(8,128)}, f32[8,8,32,128]{3,2,1,0:T(8,128)}, f32[256,256]{1,0:T(8,128)}, f32[8,16,8,128]{3,2,1,0:T(8,128)}) custom-call(s32[256]{0:T(256)} %cell.1, f32[3,8,8,32,128]{4,3,2,1,0:T(8,128)} %bitcast.13, f32[8,8,32,128]{3,2,1,0:T(8,128)} %bitcast.15, f32[8,8,32,128]{3,2,1,0:T(8,128)} %bitcast.17, ...), custom_call_target="tpu_custom_call" | custom-call | tf_op jit(solution)/shard_map/four_steps/pallas_call | solution.py:372
  93.5 0.3 all-to-all-done.1.gathered
  93.8 11.1 %all-to-all-start.2 = ((f32[128,8,128]{2,1,0:T(8,128)}), f32[128,8,128]{2,1,0:T(8,128)S(1)}, u32[]{:S(2)}, u32[]{:S(2)}) async-start(f32[128,8,128]{2,1,0:T(8,128)} %bitcast.26), calls=%async_computation.2 | async-start | bytes 1048576 | tf_op jit(solution)/shard_map/all_to_all | solution.py:613
  105.0 3.1 %product.1 = f32[256,256]{1,0:T(8,128)} custom-call(bf16[16,288,256]{2,1,0:T(8,128)(2,1)} %copy-done), custom_call_target="tpu_custom_call" | custom-call | tf_op jit(solution)/shard_map/product/pallas_call | solution.py:614
  108.0 10.8 %all-to-all-done.2.sums = f32[128,8,128]{2,1,0:T(8,128)S(1)} async-done(((f32[128,8,128]{2,1,0:T(8,128)}), f32[128,8,128]{2,1,0:T(8,128)S(1)}, u32[]{:S(2)}, u32[]{:S(2)}) %all-to-all-start.2) | async-done | bytes 524320 | tf_op jit(solution)/shard_map/all_to_all | solution.py:613
  118.9 0.8 copy-done.2
  119.7 2.3 %slip.1 = f32[8,32,256]{2,1,0:T(8,128)} custom-call(f32[256,256]{1,0:T(8,128)} %product.1, f32[128,8,128]{2,1,0:T(8,128)} %copy-done.2, f32[128,256]{1,0:T(8,128)} %constant.8.clone.phase), custom_call_target="tpu_custom_call" | custom-call | tf_op jit(solution)/shard_map/slip/pallas_call | solution.py:616
  (9 shorter events, 0.0 us)
Async XLA Ops:
  7.9 42.4 %collective-permute-start = (bf16[8,480,128]{2,1,0:T(8,128)(2,1)}, bf16[8,480,128]{2,1,0:T(8,128)(2,1)S(1)}, u32[]{:S(2)}, u32[]{:S(2)}) collective-permute-start(bf16[8,480,128]{2,1,0:T(8,128)(2,1)} %get-tuple-element.28), channel_id=1, source_target_pairs={{0,1},{1,2},{2,3},{3,4},{4,5},{5,6},{6,7},{7,8},{8,9},{9,10},{10,1... | collective-permute-start | bytes 2949128 | tf_op jit(solution)/shard_map/ppermute | solution.py:128
  12.0 38.4 %collective-permute-start.1 = (bf16[8,480,128]{2,1,0:T(8,128)(2,1)}, bf16[8,480,128]{2,1,0:T(8,128)(2,1)S(1)}, u32[]{:S(2)}, u32[]{:S(2)}) collective-permute-start(bf16[8,480,128]{2,1,0:T(8,128)(2,1)} %get-tuple-element.29), channel_id=1, source_target_pairs={{1,0},{2,1},{3,2},{4,3},{5,4},{6,5},{7,6},{8,7},{9,8},{10,9},{11,1... | collective-permute-start | bytes 2949128 | tf_op jit(solution)/shard_map/ppermute | solution.py:128
  13.3 23.2 %collective-permute-start.3 = (bf16[8,9,32,128]{3,2,1,0:T(8,128)(2,1)}, bf16[8,9,32,128]{3,2,1,0:T(8,128)(2,1)S(1)}, u32[]{:S(2)}, u32[]{:S(2)}) collective-permute-start(bf16[8,9,32,128]{3,2,1,0:T(8,128)(2,1)} %get-tuple-element.30), channel_id=1, source_target_pairs={{16,0},{32,16},{48,32},{64,48},{80,64},{96,80},{112,96},{17,1},{33... | collective-permute-start | bytes 1769480 | tf_op jit(solution)/shard_map/ppermute | solution.py:128
  16.1 20.3 %collective-permute-start.2 = (bf16[8,9,32,128]{3,2,1,0:T(8,128)(2,1)}, bf16[8,9,32,128]{3,2,1,0:T(8,128)(2,1)}, u32[]{:S(2)}, u32[]{:S(2)}) collective-permute-start(bf16[8,9,32,128]{3,2,1,0:T(8,128)(2,1)} %get-tuple-element.30), channel_id=1, source_target_pairs={{0,16},{16,32},{32,48},{48,64},{64,80},{80,96},{96,112},{1,17},{17... | collective-permute-start | bytes 1769480 | tf_op jit(solution)/shard_map/ppermute | solution.py:128
  25.7 24.7 %all-to-all-start = ((bf16[128,16,128]{2,1,0:T(8,128)(2,1)}), bf16[128,16,128]{2,1,0:T(8,128)(2,1)S(1)}, u32[]{:S(2)}, u32[]{:S(2)}) async-start(bf16[128,16,128]{2,1,0:T(8,128)(2,1)} %get-tuple-element.27), calls=%async_computation | async-start | bytes 1048576 | tf_op jit(solution)/shard_map/all_to_all | solution.py:638
  36.4 0.8 copy-start.5
  39.6 10.7 %collective-permute-start.4 = (bf16[8,72,128]{2,1,0:T(8,128)(2,1)}, bf16[8,72,128]{2,1,0:T(8,128)(2,1)S(1)}, u32[]{:S(2)}, u32[]{:S(2)}) collective-permute-start(bf16[8,72,128]{2,1,0:T(8,128)(2,1)} %get-tuple-element.32), channel_id=1, source_target_pairs={{0,1},{1,2},{2,3},{3,4},{4,5},{5,6},{6,7},{7,8},{8,9},{9,10},{10,1... | collective-permute-start | bytes 442376 | tf_op jit(solution)/shard_map/ppermute | solution.py:128
  42.9 7.5 %collective-permute-start.5 = (bf16[8,72,128]{2,1,0:T(8,128)(2,1)}, bf16[8,72,128]{2,1,0:T(8,128)(2,1)S(1)}, u32[]{:S(2)}, u32[]{:S(2)}) collective-permute-start(bf16[8,72,128]{2,1,0:T(8,128)(2,1)} %get-tuple-element.33), channel_id=1, source_target_pairs={{1,0},{2,1},{3,2},{4,3},{5,4},{6,5},{7,6},{8,7},{9,8},{10,9},{11,1... | collective-permute-start | bytes 442376 | tf_op jit(solution)/shard_map/ppermute | solution.py:128
  50.3 1.2 copy-start.1
  50.3 11.5 %copy-start.6 = (bf16[8,72,128]{2,1,0:T(8,128)(2,1)}, bf16[8,72,128]{2,1,0:T(8,128)(2,1)S(1)}, u32[]{:S(2)}) copy-start(bf16[8,72,128]{2,1,0:T(8,128)(2,1)S(1)} %collective-permute-done.4.cprev) | copy-start | bytes 442372
  50.4 4.4 %copy-start.7 = (bf16[8,72,128]{2,1,0:T(8,128)(2,1)}, bf16[8,72,128]{2,1,0:T(8,128)(2,1)S(1)}, u32[]{:S(2)}) copy-start(bf16[8,72,128]{2,1,0:T(8,128)(2,1)S(1)} %collective-permute-done.5.cnext) | copy-start | bytes 442372
  50.4 11.5 %copy-start.3 = (bf16[8,480,128]{2,1,0:T(8,128)(2,1)}, bf16[8,480,128]{2,1,0:T(8,128)(2,1)S(1)}, u32[]{:S(2)}) copy-start(bf16[8,480,128]{2,1,0:T(8,128)(2,1)S(1)} %collective-permute-done.yprev) | copy-start | bytes 2949124
  50.4 4.4 %copy-start.4 = (bf16[8,480,128]{2,1,0:T(8,128)(2,1)}, bf16[8,480,128]{2,1,0:T(8,128)(2,1)S(1)}, u32[]{:S(2)}) copy-start(bf16[8,480,128]{2,1,0:T(8,128)(2,1)S(1)} %collective-permute-done.1.ynext) | copy-start | bytes 2949124
  54.8 39.0 %all-to-all-start.1 = ((bf16[16,288,256]{2,1,0:T(8,128)(2,1)}), bf16[16,288,256]{2,1,0:T(8,128)(2,1)S(1)}, u32[]{:S(2)}, u32[]{:S(2)}) async-start(bf16[16,288,256]{2,1,0:T(8,128)(2,1)} %get-tuple-element.38), calls=%async_computation.1 | async-start | bytes 4718592 | tf_op jit(solution)/shard_map/all_to_all | solution.py:641
  93.8 11.2 %copy-start = (bf16[16,288,256]{2,1,0:T(8,128)(2,1)}, bf16[16,288,256]{2,1,0:T(8,128)(2,1)S(1)}, u32[]{:S(2)}) copy-start(bf16[16,288,256]{2,1,0:T(8,128)(2,1)S(1)} %all-to-all-done.1.gathered) | copy-start | bytes 7077892
  93.8 25.1 %all-to-all-start.2 = ((f32[128,8,128]{2,1,0:T(8,128)}), f32[128,8,128]{2,1,0:T(8,128)S(1)}, u32[]{:S(2)}, u32[]{:S(2)}) async-start(f32[128,8,128]{2,1,0:T(8,128)} %bitcast.26), calls=%async_computation.2 | async-start | bytes 1048576 | tf_op jit(solution)/shard_map/all_to_all | solution.py:613
  118.9 0.8 copy-start.2

commit v4 on v3

--- a/solution.py
+++ b/solution.py
@@ -155,7 +155,8 @@
     patch_weights,
     yprev,
     ynext,
-    side,
+    left,
+    right,
     cprev,
     cnext,
     vel_o,
@@ -210,7 +211,9 @@
                     E[BP, z, HALO + NY :] = roll(high, -1)
                     E[BP, z, HALO : HALO + NY] = roll(mid, -1)
             low, high = cp[8 * f : 8 * f + 8], cn[8 * f : 8 * f + 8]
-            mid = side[zi, f].astype(jnp.float32)
+            mid = jnp.where(
+                lane16[:NY] < 8, left[zi, f].astype(jnp.float32), right[zi, f].astype(jnp.float32)
+            )
             if f in (VX, BU):
                 to = VX if f == VX else BP
                 S[to, zi + 1, :HALO] = roll(low, -1)
@@ -378,7 +381,7 @@
             jax.ShapeDtypeStruct(spectra.shape, jnp.float32),
             jax.ShapeDtypeStruct((8, 16, 8, 128), jnp.float32),
         ),
-        in_specs=[smem] + [any_spec] * 7 + [vmem] * 9,
+        in_specs=[smem] + [any_spec] * 7 + [vmem] * 10,
         out_specs=(any_spec, any_spec, any_spec, vmem, vmem),
         scratch_shapes=[
             pltpu.VMEM((FIELDS + 1, 80, EY, 128), jnp.float32),
@@ -406,7 +409,7 @@
     return vel.reshape(velocity.shape), pr.reshape(shape), me.reshape(shape), spec, sums
 
 
-def join_kernel(left, right, side, low, high):
+def join_kernel(left, right, low, high):
     from_left = (lanes((NY, 128)) & 15) < 8
 
     def one(zi, _):
@@ -415,7 +418,6 @@
             strip = jnp.where(
                 from_left, left[zi, f].astype(jnp.float32), right[zi, f].astype(jnp.float32)
             )
-            side[zi, f] = strip.astype(jnp.bfloat16)
             lows.append(strip[:HALO])
             highs.append(strip[NY - HALO :])
         low[zi] = jnp.concatenate(lows, axis=0).astype(jnp.bfloat16)
@@ -431,9 +433,9 @@
     ynext = shifted(lo, "gy", False)
     left = shifted(q, "gx", True)
     right = shifted(q, "gx", False)
-    side, low, high = small_call(
+    low, high = small_call(
         join_kernel,
-        [(q.shape, jnp.bfloat16)] + [((8, FIELDS * HALO, 128), jnp.bfloat16)] * 2,
+        [((8, FIELDS * HALO, 128), jnp.bfloat16)] * 2,
         "join",
         (),
         0,
@@ -441,7 +443,7 @@
     )(left, right)
     cprev = shifted(high, "gy", True)
     cnext = shifted(low, "gy", False)
-    return yprev, ynext, side, cprev, cnext
+    return yprev, ynext, left, right, cprev, cnext
 
 
 def rows_of(shape):

time: 123 us -> 123 us (level)
  no operation moved by 1% of the time
where the time goes in v4:
time: 123 us
  Pallas kernels  55.9 us (45%)
  starting transfers between devices  46.3 us (38%)
  waiting for transfers between devices  16.6 us (13%)
  local copies, waits for them, and re-layouts  3.27 us (3%)
    pallas_call x1, Pallas kernels, four_steps(): pl.pallas_call(steps_kernel, out_shape=(jax.ShapeDtypeStruct((3, 8, 8, NY...  31.7 us
    ppermute x6, starting transfers between devices, shifted(): return lax.ppermute(array, axis, pairs)  16.2 us
    all_to_all x1, starting transfers between devices, slip_response(): lax.all_to_all(sums.reshape(128, 8, 128), ('gx', 'gy'), 0, 0, tiled=True)  11.3 us
    all_to_all x1, starting transfers between devices, per_device(): received = lax.all_to_all(send, ('gx', 'gy'), 0, 0, tiled=True)  11.2 us
    all_to_all x1, waiting for transfers between devices, slip_response(): lax.all_to_all(sums.reshape(128, 8, 128), ('gx', 'gy'), 0, 0, tiled=True)  10.8 us
    all_to_all x1, starting transfers between devices, per_device(): gathered = lax.all_to_all(message, 'gy', 0, 0, tiled=True)  7.59 us
    pallas_call x1, Pallas kernels, pack(): pl.pallas_call(pack_kernel, out_shape=tuple((jax.ShapeDtypeStruct(s, jnp....  7.3 us
    pallas_call x1, Pallas kernels, routed(): small_call(route_kernel, [(tiles, bf16), ((2, 128, 256), bf16), ((2, 128,...  6.09 us
  transfers between devices with their start and end apart: 9, of which 3 were waited for; matrix products, arithmetic and copies ran while one was open for 0% of the time, Pallas kernels for 35%

profile of v4, /device:TPU:1, one launch (start us, length us, event | category | flops | bytes accessed | tf_op | source)
XLA Modules:
  0.0 122.9 jit_solution(5895579363314956643)
XLA Ops:
  0.6 7.3 %pack.1 = (bf16[8,480,128]{2,1,0:T(8,128)(2,1)}, bf16[8,480,128]{2,1,0:T(8,128)(2,1)}, bf16[8,9,32,128]{3,2,1,0:T(8,128)(2,1)}) custom-call(f32[3,8,8,32,128]{4,3,2,1,0:T(8,128)} %bitcast.12, f32[8,8,32,128]{3,2,1,0:T(8,128)} %bitcast.14, f32[8,8,32,128]{3,2,1,0:T(8,128)} %bitcast.16, f32[8,8,32,128]{3,2,1,0:T(8,128)} %bitcast.18, ...), custom_call_target="tpu_custom_call" | custom-call | tf_op jit(solution)/shard_map/pack/pallas_call | solution.py:101
  7.9 4.0 %collective-permute-start = (bf16[8,480,128]{2,1,0:T(8,128)(2,1)}, bf16[8,480,128]{2,1,0:T(8,128)(2,1)S(1)}, u32[]{:S(2)}, u32[]{:S(2)}) collective-permute-start(bf16[8,480,128]{2,1,0:T(8,128)(2,1)} %get-tuple-element.27), channel_id=1, source_target_pairs={{0,1},{1,2},{2,3},{3,4},{4,5},{5,6},{6,7},{7,8},{8,9},{9,10},{10,1... | collective-permute-start | bytes 2949128 | tf_op jit(solution)/shard_map/ppermute | solution.py:128
  12.0 1.3 %collective-permute-start.1 = (bf16[8,480,128]{2,1,0:T(8,128)(2,1)}, bf16[8,480,128]{2,1,0:T(8,128)(2,1)}, u32[]{:S(2)}, u32[]{:S(2)}) collective-permute-start(bf16[8,480,128]{2,1,0:T(8,128)(2,1)} %get-tuple-element.28), channel_id=1, source_target_pairs={{1,0},{2,1},{3,2},{4,3},{5,4},{6,5},{7,6},{8,7},{9,8},{10,9},{11,1... | collective-permute-start | bytes 2949128 | tf_op jit(solution)/shard_map/ppermute | solution.py:128
  13.3 2.9 %collective-permute-start.3 = (bf16[8,9,32,128]{3,2,1,0:T(8,128)(2,1)}, bf16[8,9,32,128]{3,2,1,0:T(8,128)(2,1)S(1)}, u32[]{:S(2)}, u32[]{:S(2)}) collective-permute-start(bf16[8,9,32,128]{3,2,1,0:T(8,128)(2,1)} %get-tuple-element.29), channel_id=1, source_target_pairs={{16,0},{32,16},{48,32},{64,48},{80,64},{96,80},{112,96},{17,1},{33... | collective-permute-start | bytes 1769480 | tf_op jit(solution)/shard_map/ppermute | solution.py:128
  16.1 3.4 %collective-permute-start.2 = (bf16[8,9,32,128]{3,2,1,0:T(8,128)(2,1)}, bf16[8,9,32,128]{3,2,1,0:T(8,128)(2,1)S(1)}, u32[]{:S(2)}, u32[]{:S(2)}) collective-permute-start(bf16[8,9,32,128]{3,2,1,0:T(8,128)(2,1)} %get-tuple-element.29), channel_id=1, source_target_pairs={{0,16},{16,32},{32,48},{48,64},{64,80},{80,96},{96,112},{1,17},{17... | collective-permute-start | bytes 1769480 | tf_op jit(solution)/shard_map/ppermute | solution.py:128
  19.6 6.1 %route.1 = (bf16[128,16,128]{2,1,0:T(8,128)(2,1)}, bf16[2,128,256]{2,1,0:T(8,128)(2,1)}, bf16[2,128,256]{2,1,0:T(8,128)(2,1)}, bf16[256,128]{1,0:T(8,128)(2,1)}, bf16[16,32,256]{2,1,0:T(8,128)(2,1)}) custom-call(s32[64,512]{1,0:T(8,128)} %table.1, f32[256,256]{1,0:T(8,128)} %spectra.2, bf16[256,512]{1,0:T(8,128)(2,1)} %bitcast.27), custom_call_target="tpu_custom_call" | custom-call | tf_op jit(solution)/shard_map/route/pallas_call | solution.py:585
  25.7 11.2 %all-to-all-start = ((bf16[128,16,128]{2,1,0:T(8,128)(2,1)}), bf16[128,16,128]{2,1,0:T(8,128)(2,1)S(1)}, u32[]{:S(2)}, u32[]{:S(2)}) async-start(bf16[128,16,128]{2,1,0:T(8,128)(2,1)} %get-tuple-element.26), calls=%async_computation | async-start | bytes 1048576 | tf_op jit(solution)/shard_map/all_to_all | solution.py:640
  36.9 0.0 collective-permute-done.3.right
  36.9 0.0 copy-start.1
  36.9 0.0 collective-permute-done.2.left
  36.9 0.8 copy-done.1
  37.8 0.8 copy-done.2
  38.6 2.0 %join.1 = (bf16[8,72,128]{2,1,0:T(8,128)(2,1)}, bf16[8,72,128]{2,1,0:T(8,128)(2,1)}) custom-call(bf16[8,9,32,128]{3,2,1,0:T(8,128)(2,1)} %copy-done.2, bf16[8,9,32,128]{3,2,1,0:T(8,128)(2,1)} %copy-done.1), custom_call_target="tpu_custom_call" | custom-call | tf_op jit(solution)/shard_map/join/pallas_call | solution.py:436
  40.6 3.3 %collective-permute-start.4 = (bf16[8,72,128]{2,1,0:T(8,128)(2,1)}, bf16[8,72,128]{2,1,0:T(8,128)(2,1)S(1)}, u32[]{:S(2)}, u32[]{:S(2)}) collective-permute-start(bf16[8,72,128]{2,1,0:T(8,128)(2,1)} %get-tuple-element.30), channel_id=1, source_target_pairs={{0,1},{1,2},{2,3},{3,4},{4,5},{5,6},{6,7},{7,8},{8,9},{9,10},{10,1... | collective-permute-start | bytes 442376 | tf_op jit(solution)/shard_map/ppermute | solution.py:128
  43.9 1.3 %collective-permute-start.5 = (bf16[8,72,128]{2,1,0:T(8,128)(2,1)}, bf16[8,72,128]{2,1,0:T(8,128)(2,1)S(1)}, u32[]{:S(2)}, u32[]{:S(2)}) collective-permute-start(bf16[8,72,128]{2,1,0:T(8,128)(2,1)} %get-tuple-element.31), channel_id=1, source_target_pairs={{1,0},{2,1},{3,2},{4,3},{5,4},{6,5},{7,6},{8,7},{9,8},{10,9},{11,1... | collective-permute-start | bytes 442376 | tf_op jit(solution)/shard_map/ppermute | solution.py:128
  45.2 5.6 %all-to-all-done.received = bf16[128,16,128]{2,1,0:T(8,128)(2,1)S(1)} async-done(((bf16[128,16,128]{2,1,0:T(8,128)(2,1)}), bf16[128,16,128]{2,1,0:T(8,128)(2,1)S(1)}, u32[]{:S(2)}, u32[]{:S(2)}) %all-to-all-start) | async-done | bytes 524320 | tf_op jit(solution)/shard_map/all_to_all | solution.py:640
  50.8 0.0 collective-permute-done.4.cprev
  50.8 0.0 collective-permute-done.5.cnext
  50.8 0.0 copy-start.7
  50.9 0.0 collective-permute-done.yprev
  50.9 0.0 collective-permute-done.1.ynext
  50.9 0.8 copy-done.3
  51.7 3.3 %sort.1 = (bf16[16,288,256]{2,1,0:T(8,128)(2,1)}, bf16[256,512]{1,0:T(8,128)(2,1)}) custom-call(bf16[128,16,128]{2,1,0:T(8,128)(2,1)} %copy-done.3, bf16[2,128,256]{2,1,0:T(8,128)(2,1)} %get-tuple-element.33.place, bf16[2,128,256]{2,1,0:T(8,128)(2,1)} %get-tuple-element.34.pick, bf16[16,32,256]{2,1,0:T(8,128)(2,1)} %get-tuple-element.35.turned), custom_call_target="tpu_custom_call" | custom-call | tf_op jit(solution)/shard_map/sort/pallas_call | solution.py:602
  55.0 7.6 %all-to-all-start.1 = ((bf16[16,288,256]{2,1,0:T(8,128)(2,1)}), bf16[16,288,256]{2,1,0:T(8,128)(2,1)S(1)}, u32[]{:S(2)}, u32[]{:S(2)}) async-start(bf16[16,288,256]{2,1,0:T(8,128)(2,1)} %get-tuple-element.36), calls=%async_computation.1 | async-start | bytes 4718592 | tf_op jit(solution)/shard_map/all_to_all | solution.py:643
  62.6 31.7 %four_steps.1 = (f32[3,8,8,32,128]{4,3,2,1,0:T(8,128)}, f32[8,8,32,128]{3,2,1,0:T(8,128)}, f32[8,8,32,128]{3,2,1,0:T(8,128)}, f32[256,256]{1,0:T(8,128)}, f32[8,16,8,128]{3,2,1,0:T(8,128)}) custom-call(s32[256]{0:T(256)} %cell.1, f32[3,8,8,32,128]{4,3,2,1,0:T(8,128)} %bitcast.13, f32[8,8,32,128]{3,2,1,0:T(8,128)} %bitcast.15, f32[8,8,32,128]{3,2,1,0:T(8,128)} %bitcast.17, ...), custom_call_target="tpu_custom_call" | custom-call | tf_op jit(solution)/shard_map/four_steps/pallas_call | solution.py:375
  94.3 0.1 all-to-all-done.1.gathered
  94.5 11.3 %all-to-all-start.2 = ((f32[128,8,128]{2,1,0:T(8,128)}), f32[128,8,128]{2,1,0:T(8,128)S(1)}, u32[]{:S(2)}, u32[]{:S(2)}) async-start(f32[128,8,128]{2,1,0:T(8,128)} %bitcast.26), calls=%async_computation.2 | async-start | bytes 1048576 | tf_op jit(solution)/shard_map/all_to_all | solution.py:615
  105.8 0.0 copy-done
  105.8 3.1 %product.1 = f32[256,256]{1,0:T(8,128)} custom-call(bf16[16,288,256]{2,1,0:T(8,128)(2,1)} %copy-done), custom_call_target="tpu_custom_call" | custom-call | tf_op jit(solution)/shard_map/product/pallas_call | solution.py:616
  108.9 10.8 %all-to-all-done.2.sums = f32[128,8,128]{2,1,0:T(8,128)S(1)} async-done(((f32[128,8,128]{2,1,0:T(8,128)}), f32[128,8,128]{2,1,0:T(8,128)S(1)}, u32[]{:S(2)}, u32[]{:S(2)}) %all-to-all-start.2) | async-done | bytes 524320 | tf_op jit(solution)/shard_map/all_to_all | solution.py:615
  119.7 0.8 copy-done.4
  120.5 2.3 %slip.1 = f32[8,32,256]{2,1,0:T(8,128)} custom-call(f32[256,256]{1,0:T(8,128)} %product.1, f32[128,8,128]{2,1,0:T(8,128)} %copy-done.4, f32[128,256]{1,0:T(8,128)} %constant.8.clone.phase), custom_call_target="tpu_custom_call" | custom-call | tf_op jit(solution)/shard_map/slip/pallas_call | solution.py:618
  (9 shorter events, 0.0 us)
Async XLA Ops:
  7.9 42.9 %collective-permute-start = (bf16[8,480,128]{2,1,0:T(8,128)(2,1)}, bf16[8,480,128]{2,1,0:T(8,128)(2,1)S(1)}, u32[]{:S(2)}, u32[]{:S(2)}) collective-permute-start(bf16[8,480,128]{2,1,0:T(8,128)(2,1)} %get-tuple-element.27), channel_id=1, source_target_pairs={{0,1},{1,2},{2,3},{3,4},{4,5},{5,6},{6,7},{7,8},{8,9},{9,10},{10,1... | collective-permute-start | bytes 2949128 | tf_op jit(solution)/shard_map/ppermute | solution.py:128
  12.0 38.9 %collective-permute-start.1 = (bf16[8,480,128]{2,1,0:T(8,128)(2,1)}, bf16[8,480,128]{2,1,0:T(8,128)(2,1)}, u32[]{:S(2)}, u32[]{:S(2)}) collective-permute-start(bf16[8,480,128]{2,1,0:T(8,128)(2,1)} %get-tuple-element.28), channel_id=1, source_target_pairs={{1,0},{2,1},{3,2},{4,3},{5,4},{6,5},{7,6},{8,7},{9,8},{10,9},{11,1... | collective-permute-start | bytes 2949128 | tf_op jit(solution)/shard_map/ppermute | solution.py:128
  13.3 23.7 %collective-permute-start.3 = (bf16[8,9,32,128]{3,2,1,0:T(8,128)(2,1)}, bf16[8,9,32,128]{3,2,1,0:T(8,128)(2,1)S(1)}, u32[]{:S(2)}, u32[]{:S(2)}) collective-permute-start(bf16[8,9,32,128]{3,2,1,0:T(8,128)(2,1)} %get-tuple-element.29), channel_id=1, source_target_pairs={{16,0},{32,16},{48,32},{64,48},{80,64},{96,80},{112,96},{17,1},{33... | collective-permute-start | bytes 1769480 | tf_op jit(solution)/shard_map/ppermute | solution.py:128
  16.1 20.8 %collective-permute-start.2 = (bf16[8,9,32,128]{3,2,1,0:T(8,128)(2,1)}, bf16[8,9,32,128]{3,2,1,0:T(8,128)(2,1)S(1)}, u32[]{:S(2)}, u32[]{:S(2)}) collective-permute-start(bf16[8,9,32,128]{3,2,1,0:T(8,128)(2,1)} %get-tuple-element.29), channel_id=1, source_target_pairs={{0,16},{16,32},{32,48},{48,64},{64,80},{80,96},{96,112},{1,17},{17... | collective-permute-start | bytes 1769480 | tf_op jit(solution)/shard_map/ppermute | solution.py:128
  25.7 25.2 %all-to-all-start = ((bf16[128,16,128]{2,1,0:T(8,128)(2,1)}), bf16[128,16,128]{2,1,0:T(8,128)(2,1)S(1)}, u32[]{:S(2)}, u32[]{:S(2)}) async-start(bf16[128,16,128]{2,1,0:T(8,128)(2,1)} %get-tuple-element.26), calls=%async_computation | async-start | bytes 1048576 | tf_op jit(solution)/shard_map/all_to_all | solution.py:640
  36.9 0.8 copy-start.1
  37.8 0.8 copy-start.2
  40.6 10.2 %collective-permute-start.4 = (bf16[8,72,128]{2,1,0:T(8,128)(2,1)}, bf16[8,72,128]{2,1,0:T(8,128)(2,1)S(1)}, u32[]{:S(2)}, u32[]{:S(2)}) collective-permute-start(bf16[8,72,128]{2,1,0:T(8,128)(2,1)} %get-tuple-element.30), channel_id=1, source_target_pairs={{0,1},{1,2},{2,3},{3,4},{4,5},{5,6},{6,7},{7,8},{8,9},{9,10},{10,1... | collective-permute-start | bytes 442376 | tf_op jit(solution)/shard_map/ppermute | solution.py:128
  43.9 6.9 %collective-permute-start.5 = (bf16[8,72,128]{2,1,0:T(8,128)(2,1)}, bf16[8,72,128]{2,1,0:T(8,128)(2,1)S(1)}, u32[]{:S(2)}, u32[]{:S(2)}) collective-permute-start(bf16[8,72,128]{2,1,0:T(8,128)(2,1)} %get-tuple-element.31), channel_id=1, source_target_pairs={{1,0},{2,1},{3,2},{4,3},{5,4},{6,5},{7,6},{8,7},{9,8},{10,9},{11,1... | collective-permute-start | bytes 442376 | tf_op jit(solution)/shard_map/ppermute | solution.py:128
  50.8 0.8 copy-start.3
  50.8 11.7 %copy-start.6 = (bf16[8,72,128]{2,1,0:T(8,128)(2,1)}, bf16[8,72,128]{2,1,0:T(8,128)(2,1)S(1)}, u32[]{:S(2)}) copy-start(bf16[8,72,128]{2,1,0:T(8,128)(2,1)S(1)} %collective-permute-done.4.cprev) | copy-start | bytes 442372
  50.8 4.1 %copy-start.7 = (bf16[8,72,128]{2,1,0:T(8,128)(2,1)}, bf16[8,72,128]{2,1,0:T(8,128)(2,1)S(1)}, u32[]{:S(2)}) copy-start(bf16[8,72,128]{2,1,0:T(8,128)(2,1)S(1)} %collective-permute-done.5.cnext) | copy-start | bytes 442372
  50.9 11.7 %copy-start.5 = (bf16[8,480,128]{2,1,0:T(8,128)(2,1)}, bf16[8,480,128]{2,1,0:T(8,128)(2,1)S(1)}, u32[]{:S(2)}) copy-start(bf16[8,480,128]{2,1,0:T(8,128)(2,1)S(1)} %collective-permute-done.yprev) | copy-start | bytes 2949124
  55.0 39.5 %all-to-all-start.1 = ((bf16[16,288,256]{2,1,0:T(8,128)(2,1)}), bf16[16,288,256]{2,1,0:T(8,128)(2,1)S(1)}, u32[]{:S(2)}, u32[]{:S(2)}) async-start(bf16[16,288,256]{2,1,0:T(8,128)(2,1)} %get-tuple-element.36), calls=%async_computation.1 | async-start | bytes 4718592 | tf_op jit(solution)/shard_map/all_to_all | solution.py:643
  94.5 11.3 %copy-start = (bf16[16,288,256]{2,1,0:T(8,128)(2,1)}, bf16[16,288,256]{2,1,0:T(8,128)(2,1)S(1)}, u32[]{:S(2)}) copy-start(bf16[16,288,256]{2,1,0:T(8,128)(2,1)S(1)} %all-to-all-done.1.gathered) | copy-start | bytes 7077892
  94.5 25.2 %all-to-all-start.2 = ((f32[128,8,128]{2,1,0:T(8,128)}), f32[128,8,128]{2,1,0:T(8,128)S(1)}, u32[]{:S(2)}, u32[]{:S(2)}) async-start(f32[128,8,128]{2,1,0:T(8,128)} %bitcast.26), calls=%async_computation.2 | async-start | bytes 1048576 | tf_op jit(solution)/shard_map/all_to_all | solution.py:615
  119.7 0.8 copy-start.4
